TPU v7x, 32 devices: a whole 2x2x4 slice. The times are simulated.
32 devices in a mesh: wide: 16 (over z, y, core), narrow: 2 (over x).
Axes of the slice: x: 2, y: 2, z: 4, core: 2. Of those that a mesh axis runs over, the one named last changes fastest.
Arguments:
- latent: bfloat16 [16, 64, 128], P(None, 'wide'), may hold values from -6 to 6
- land_sea: int32 [64, 128], P('wide'), may hold values 0 or 1
- head_shift: int32 [16, 2], P('narrow'), may hold values from -1 to 1
- logit_scale: float32 [16], P('narrow'), may hold values from 4 to 600
- embed_weight: bfloat16 [16, 1024], replicated, may hold values from -1.5 to 1.5
- land_vector: bfloat16 [1024], replicated, may hold values from -6 to 6
- qkv_weight: bfloat16 [1024, 3, 1024], P(None, None, 'narrow'), may hold values from -0.1875 to 0.1875
- out_weight: bfloat16 [1024, 1024], P('narrow'), may hold values from -0.75 to 0.75
- proj_weight: bfloat16 [1024, 16], replicated, may hold values from -0.1875 to 0.1875
- conv_in_weight: bfloat16 [3, 3, 16, 512], replicated, may hold values from -0.5 to 0.5
- level_one_weight: bfloat16 [3, 3, 512, 512], replicated, may hold values from -0.15625 to 0.15625
- level_two_weight: bfloat16 [3, 3, 512, 256], replicated, may hold values from -0.15625 to 0.15625
- level_three_weight: bfloat16 [3, 3, 256, 128], replicated, may hold values from -0.21875 to 0.21875
- conv_out_weight: bfloat16 [3, 3, 128, 4], replicated, may hold values from -0.3125 to 0.3125
Outputs:
- image: float32 [4, 512, 1024], P(None, 'wide', 'narrow')
All inputs are finite; a program needn't handle non-finite values. No bound on the sum of `land_sea` on one device may be relied on, other than what follows from the above.
Results may differ from a plain program's by a relative error of at most 0.025.
Values may be sent and summed in bfloat16 or wider, within the bound.
A program may use at most 256 MiB of HBM per device.

v0:
```python
import math

import jax
import jax.numpy as jnp
from jax import lax
from jax.sharding import PartitionSpec as P

WIN = 7


plan_now = 0.3
plan_next = 0.5
keep_factor = math.sqrt(plan_next / plan_now)
noise_factor = math.sqrt(1.0 - plan_next) - keep_factor * math.sqrt(1.0 - plan_now)


def extended(cells, sides, width):
    for axis, dim in sides:
        count = lax.axis_size(axis)
        ends = count - 1
        head = lax.slice_in_dim(cells, 0, width, axis=dim)
        tail = lax.slice_in_dim(cells, cells.shape[dim] - width, cells.shape[dim], axis=dim)
        cells = jnp.concatenate(
            [
                lax.ppermute(tail, axis, [(i, (i + 1) % count) for i in range(ends)]),
                cells,
                lax.ppermute(head, axis, [((i + 1) % count, i) for i in range(ends)]),
            ],
            axis=dim,
        )
    return cells


def unit_rows(values_in):
    return values_in * lax.rsqrt(jnp.sum(values_in * values_in, axis=1, keepdims=True) + 1e-06)


def window_attend(query_hat, key_pad, value_pad, valid_cells, shifts, scales):
    row_count = query_hat.shape[2]
    col_count = query_hat.shape[3]
    reach = (WIN - 1) // 2
    margin = reach + 1
    offsets = [
        (row_step, col_step)
        for row_step in range(-reach, reach + 1)
        for col_step in range(-reach, reach + 1)
    ]

    def attend_head(query_head, key_head, value_head, shift_pair, scale_head):
        head_dim = query_head.shape[0]
        anchor = jnp.zeros((), jnp.int32)
        shift_row = shift_pair[0]
        shift_col = shift_pair[1]
        scores = []
        for row_step, col_step in offsets:
            row_start = shift_row + (margin + row_step)
            col_start = shift_col + (margin + col_step)
            key_block = lax.dynamic_slice(
                key_head, (anchor, row_start, col_start), (head_dim, row_count, col_count)
            )
            inside = lax.dynamic_slice(valid_cells, (row_start, col_start), (row_count, col_count))
            scores.append(
                jnp.where(inside, scale_head * jnp.sum(query_head * key_block, axis=0), -jnp.inf)
            )
        scores = jnp.stack(scores)
        row_peak = jnp.max(scores, axis=0)
        exponent = jnp.exp(scores - row_peak)
        weights = (exponent / jnp.sum(exponent, axis=0)).astype(jnp.bfloat16)
        accumulated = jnp.zeros((head_dim, row_count, col_count), jnp.float32)
        for slot_index, (row_step, col_step) in enumerate(offsets):
            row_start = shift_row + (margin + row_step)
            col_start = shift_col + (margin + col_step)
            value_block = lax.dynamic_slice(
                value_head, (anchor, row_start, col_start), (head_dim, row_count, col_count)
            )
            accumulated = accumulated + weights[slot_index].astype(
                jnp.float32
            ) * value_block.astype(jnp.float32)
        return accumulated.astype(jnp.bfloat16)

    return jax.vmap(attend_head)(query_hat, key_pad, value_pad, shifts, scales)


def widen(field_in):
    row_count, col_count, channels = field_in.shape
    grown = jnp.broadcast_to(field_in[:, None, :, None, :], (row_count, 2, col_count, 2, channels))
    return grown.reshape(2 * row_count, 2 * col_count, channels)


def conv_valid(padded, weight):
    return lax.conv_general_dilated(
        padded[None],
        weight,
        (1, 1),
        "VALID",
        dimension_numbers=("NHWC", "HWIO", "NHWC"),
        preferred_element_type=jnp.float32,
    )[0]


def conv_final(padded, weight):
    return lax.conv_general_dilated(
        padded[None],
        weight,
        (1, 1),
        "VALID",
        dimension_numbers=("NHWC", "HWIO", "NCHW"),
        preferred_element_type=jnp.float32,
    )[0]


def tile_padded(field_in):
    return extended(field_in, (("wide", 0), ("narrow", 1)), 1)


def level_conv(field_in, weight):
    padded = extended(widen(field_in), (("wide", 0), ("narrow", 1)), 1)
    return conv_valid(padded, weight)


def shards(
    latent,
    land_sea,
    head_shift,
    logit_scale,
    embed_weight,
    land_vector,
    qkv_weight,
    out_weight,
    proj_weight,
    conv_in_weight,
    level_one_weight,
    level_two_weight,
    level_three_weight,
    conv_out_weight,
):
    channels, row_count, col_count = latent.shape
    margin = (WIN - 1) // 2 + 1
    heads_here = head_shift.shape[0]
    head_dim = qkv_weight.shape[2] // heads_here
    land_cells = land_sea.astype(jnp.bfloat16)

    def project(part_index, field_in):
        flat_proj = jnp.einsum(
            "dm,drw->mrw", qkv_weight[:, part_index], field_in, preferred_element_type=jnp.float32
        )
        return flat_proj.reshape(heads_here, head_dim, field_in.shape[1], col_count)

    mixed_rows = jnp.einsum("cd,crw->drw", embed_weight, latent, preferred_element_type=jnp.float32)
    mixed_rows = (
        mixed_rows
        + land_cells.astype(jnp.float32)[None] * land_vector.astype(jnp.float32)[:, None, None]
    )
    embedded = mixed_rows.astype(jnp.bfloat16)
    query_hat = unit_rows(project(0, embedded))
    key_hat = unit_rows(project(1, embedded))
    values = project(2, embedded).astype(jnp.bfloat16)
    key_value = jnp.stack([key_hat, values.astype(jnp.float32)])
    key_value = extended(key_value, (("wide", 3),), margin)
    key_ext = key_value[0]
    value_ext = key_value[1].astype(jnp.bfloat16)
    pad_spec = ((0, 0), (0, 0), (0, 0), (margin, margin))
    key_pad = jnp.pad(key_ext, pad_spec)
    value_pad = jnp.pad(value_ext, pad_spec)
    band_start = lax.axis_index("wide") * row_count
    total_rows = row_count * lax.axis_size("wide")
    row_index = band_start + jnp.arange(row_count + 2 * margin, dtype=jnp.int32) - margin
    col_index = jnp.arange(col_count + 2 * margin, dtype=jnp.int32) - margin
    row_inside = (row_index >= 0) & (row_index < total_rows)
    col_inside = (col_index >= 0) & (col_index < col_count)
    valid_cells = row_inside[:, None] & col_inside[None, :]
    heads_out = window_attend(query_hat, key_pad, value_pad, valid_cells, head_shift, logit_scale)
    mixed_heads = heads_out.reshape(heads_here * head_dim, row_count, col_count)
    attended_part = jnp.einsum(
        "md,mrw->drw", out_weight, mixed_heads, preferred_element_type=jnp.float32
    )
    noise_part = jnp.einsum(
        "dc,drw->crw",
        proj_weight.astype(jnp.float32),
        attended_part,
        precision=lax.Precision.HIGHEST,
    )
    tile_cols = col_count // lax.axis_size("narrow")
    col_start = lax.axis_index("narrow") * tile_cols
    noise_all = lax.psum(noise_part.astype(jnp.bfloat16), "narrow").astype(jnp.float32)
    noise_tile = lax.dynamic_slice_in_dim(noise_all, col_start, tile_cols, 2)
    embedded_tile = lax.dynamic_slice_in_dim(embedded, col_start, tile_cols, 2)
    latent_tile = lax.dynamic_slice_in_dim(latent, col_start, tile_cols, 2)
    noise_tile = noise_tile + jnp.einsum(
        "dc,drw->crw", proj_weight, embedded_tile, preferred_element_type=jnp.float32
    )
    stepped = (keep_factor * latent_tile.astype(jnp.float32) + noise_factor * noise_tile).astype(
        jnp.bfloat16
    )
    stepped_cells = jnp.transpose(stepped, (1, 2, 0))
    hidden = jax.nn.silu(conv_valid(tile_padded(stepped_cells), conv_in_weight)).astype(
        jnp.bfloat16
    )
    for weight in (level_one_weight, level_two_weight, level_three_weight):
        hidden = jax.nn.silu(level_conv(hidden, weight)).astype(jnp.bfloat16)
    return conv_final(tile_padded(hidden), conv_out_weight)


def solution(mesh):
    in_specs = (
        P(None, "wide", None),
        P("wide", None),
        P("narrow", None),
        P("narrow"),
        P(),
        P(),
        P(None, None, "narrow"),
        P("narrow", None),
        P(),
        P(),
        P(),
        P(),
        P(),
        P(),
    )
    out_specs = P(None, "wide", "narrow")
    return jax.shard_map(shards, mesh=mesh, in_specs=in_specs, out_specs=out_specs, check_vma=False)
```

profile of v0, /device:TPU:21, one launch (start us, length us, event | category | flops | bytes accessed | tf_op | source)
XLA Modules:
  0.0 2370.7 jit_solution(14593110319047477048)
XLA Ops:
  49.5 21.3 while.92
  71.6 21.3 while.90
  93.7 20.9 while.91
  115.4 20.9 while.49
  137.1 21.0 while.97
  158.9 21.2 while.50
  180.9 21.4 while.51
  203.1 17.2 while.52
  221.1 16.0 while.53
  237.9 16.0 while.54
  254.7 16.8 while.55
  272.2 16.5 while.56
  289.6 16.0 while.57
  306.4 15.4 while.96
  322.6 16.5 while.58
  339.8 16.5 while.59
  357.1 15.8 while.60
  373.7 15.8 while.61
  390.3 15.8 while.62
  406.9 16.5 while.63
  424.2 16.5 while.64
  441.5 16.6 while.65
  458.8 16.6 while.95
  476.2 16.4 while.66
  493.3 16.4 while.67
  510.5 16.4 while.68
  527.7 15.2 while.69
  543.7 15.4 while.70
  559.9 16.1 while.71
  576.8 16.1 while.72
  593.7 16.7 while.73
  611.2 16.7 while.94
  628.7 14.9 while.74
  644.3 16.3 while.75
  661.6 16.3 while.76
  678.6 16.2 while.77
  695.6 16.2 while.78
  712.7 16.3 while.79
  729.7 17.1 while.80
  747.5 17.1 while.81
  765.4 17.1 while.93
  783.2 17.1 while.82
  801.1 17.2 while.83
  819.0 16.2 while.84
  836.1 16.3 while.85
  853.1 16.5 while.86
  870.3 16.1 while.87
  887.2 16.8 while.88
  904.8 15.8 while.89
  1193.2 22.9 multiply_reduce_fusion
  1218.1 15.1 multiply_reduce_fusion.36
  1355.5 21.2 multiply_reduce_fusion.18
  1977.7 12.9 add_add_fusion
  1993.8 12.1 fusion.62
  2059.6 8.0 fusion.42
  2105.5 8.3 reshape.2293
  2118.6 11.2 broadcast_select_fusion.1
  2138.6 13.1 reshape.1345
  2176.7 8.7 maximum_bitcast_fusion
  2185.4 7.6 pad.114
  2193.1 14.0 reshape.2300
  2207.0 10.0 copy.1123
  2218.1 24.7 %broadcast_select_fusion = f32[32,8,65,128]{3,1,2,0:T(8,128)S(1)} fusion(pred[8,65]{0,1:T(8,128)(4,1)S(1)} %copy-done.209, bf16[3,3,256,128]{3,2,1,0:T(8,128)(2,1)S(1)} %copy-done.207, bf16[34,1,7,2,256]{4,2,3,0,1:T(8,128)(2,1)S(1)} %slice.1319, bf16[34,1,8,65,256]{4,2,3,0,1:T(8,128)(2,1)} %copy.1123), kind=kOutput, calls=%fused_computation.229 | convolution fusion | flops 9844793344 | bytes 18405896 | tf_op jit(solution)/shard_map/conv_general_dilated | solution.py:91
  2270.6 95.1 %broadcast_select_fusion.2 = f32[32,8,65,4]{1,3,2,0:T(4,128)} fusion(pred[8,65]{0,1:T(8,128)(4,1)S(1)} %copy-done.209, bf16[3,3,128,4]{2,3,1,0:T(4,128)(2,1)S(1)} %copy-done.208, bf16[34,1,7,2,128]{4,2,3,0,1:T(8,128)(2,1)S(1)} %slice.1323, bf16[34,1,8,65,128]{4,2,3,0,1:T(8,128)(2,1)S(1)} %copy.1127), kind=kOutput, calls=%fused_computation.239 | convolution fusion | flops 167416832 | bytes 4923912 | tf_op jit(solution)/shard_map/conv_general_dilated | solution.py:102
  (2225 shorter events, 2082.1 us)
Async XLA Ops:
  0.0 2118.6 %copy-start = (bf16[3,3,512,256]{3,2,1,0:T(8,128)(2,1)S(1)}, bf16[3,3,512,256]{3,2,1,0:T(8,128)(2,1)}, u32[]{:S(2)}) copy-start(bf16[3,3,512,256]{3,2,1,0:T(8,128)(2,1)} %param.25) | copy-start | bytes 7077892
  28.3 894.2 %collective-permute-start.1 = (f32[2,8,64,4,128]{4,2,3,1,0:T(8,128)}, f32[2,8,64,4,128]{4,2,3,1,0:T(8,128)}, u32[]{:S(2)}, u32[]{:S(2)}) collective-permute-start(f32[2,8,64,4,128]{4,2,3,1,0:T(8,128)} %copy.825), channel_id=1, source_target_pairs={{2,0},{4,2},{6,4},{8,6},{10,8},{12,10},{14,12},{16,14},{18,16},{20... | collective-permute-start | bytes 6291464 | tf_op jit(solution)/shard_map/ppermute | solution.py:27
  31.0 895.3 %collective-permute-start = (f32[2,8,64,4,128]{4,2,3,1,0:T(8,128)}, f32[2,8,64,4,128]{4,2,3,1,0:T(8,128)}, u32[]{:S(2)}, u32[]{:S(2)}) collective-permute-start(f32[2,8,64,4,128]{4,2,3,1,0:T(8,128)} %copy.825), channel_id=1, source_target_pairs={{0,2},{2,4},{4,6},{6,8},{8,10},{10,12},{12,14},{14,16},{16,18},{18... | collective-permute-start | bytes 6291464 | tf_op jit(solution)/shard_map/ppermute | solution.py:25
  39.8 1148.5 %copy-start.20 = (s32[8]{0:T(128)}, s32[8]{0:T(128)S(1)}, u32[]{:S(2)}) copy-start(s32[8]{0:T(128)S(1)} %get-tuple-element.1045) | copy-start | bytes 100
  47.9 258.5 %copy-start.164 = (s32[8,2]{0,1:T(2,128)S(1)}, s32[8,2]{0,1:T(2,128)}, u32[]{:S(2)}) copy-start(s32[8,2]{0,1:T(2,128)} %get-tuple-element.2820) | copy-start | bytes 196
  47.9 274.7 %copy-start.163 = (s32[8,2]{0,1:T(2,128)S(1)}, s32[8,2]{0,1:T(2,128)}, u32[]{:S(2)}) copy-start(s32[8,2]{0,1:T(2,128)} %get-tuple-element.2835) | copy-start | bytes 196
  48.8 291.1 %copy-start.162 = (s32[8,2]{0,1:T(2,128)S(1)}, s32[8,2]{0,1:T(2,128)}, u32[]{:S(2)}) copy-start(s32[8,2]{0,1:T(2,128)} %get-tuple-element.2850) | copy-start | bytes 196
  70.8 286.3 %copy-start.111 = (pred[8,4,128]{2,1,0:T(4,128)(4,1)}, pred[8,4,128]{2,1,0:T(4,128)(4,1)S(1)}, u32[]{:S(2)}) copy-start(pred[8,4,128]{2,1,0:T(4,128)(4,1)S(1)} %get-tuple-element.356) | copy-start | bytes 12292
  70.8 286.3 %copy-start.161 = (s32[8,2]{0,1:T(2,128)S(1)}, s32[8,2]{0,1:T(2,128)}, u32[]{:S(2)}) copy-start(s32[8,2]{0,1:T(2,128)} %get-tuple-element.2865) | copy-start | bytes 196
  92.9 280.8 %copy-start.113 = (pred[8,4,128]{2,1,0:T(4,128)(4,1)}, pred[8,4,128]{2,1,0:T(4,128)(4,1)S(1)}, u32[]{:S(2)}) copy-start(pred[8,4,128]{2,1,0:T(4,128)(4,1)S(1)} %get-tuple-element.340) | copy-start | bytes 12292
  114.6 275.7 %copy-start.115 = (pred[8,4,128]{2,1,0:T(4,128)(4,1)}, pred[8,4,128]{2,1,0:T(4,128)(4,1)S(1)}, u32[]{:S(2)}) copy-start(pred[8,4,128]{2,1,0:T(4,128)(4,1)S(1)} %get-tuple-element.348) | copy-start | bytes 12292
  136.3 270.6 %copy-start.116 = (pred[8,4,128]{2,1,0:T(4,128)(4,1)}, pred[8,4,128]{2,1,0:T(4,128)(4,1)S(1)}, u32[]{:S(2)}) copy-start(pred[8,4,128]{2,1,0:T(4,128)(4,1)S(1)} %get-tuple-element.12) | copy-start | bytes 12292
  136.3 270.6 %copy-start.180 = (s32[8,2]{0,1:T(2,128)S(1)}, s32[8,2]{0,1:T(2,128)}, u32[]{:S(2)}) copy-start(s32[8,2]{0,1:T(2,128)} %get-tuple-element.2910) | copy-start | bytes 196
  158.1 266.1 %copy-start.117 = (pred[8,4,128]{2,1,0:T(4,128)(4,1)}, pred[8,4,128]{2,1,0:T(4,128)(4,1)S(1)}, u32[]{:S(2)}) copy-start(pred[8,4,128]{2,1,0:T(4,128)(4,1)S(1)} %get-tuple-element.396) | copy-start | bytes 12292
  180.1 261.3 %copy-start.118 = (pred[8,4,128]{2,1,0:T(4,128)(4,1)}, pred[8,4,128]{2,1,0:T(4,128)(4,1)S(1)}, u32[]{:S(2)}) copy-start(pred[8,4,128]{2,1,0:T(4,128)(4,1)S(1)} %get-tuple-element.20) | copy-start | bytes 12292
  180.1 261.3 %copy-start.179 = (s32[8,2]{0,1:T(2,128)S(1)}, s32[8,2]{0,1:T(2,128)}, u32[]{:S(2)}) copy-start(s32[8,2]{0,1:T(2,128)} %get-tuple-element.2940) | copy-start | bytes 196
  202.3 256.5 %copy-start.119 = (pred[8,4,128]{2,1,0:T(4,128)(4,1)}, pred[8,4,128]{2,1,0:T(4,128)(4,1)S(1)}, u32[]{:S(2)}) copy-start(pred[8,4,128]{2,1,0:T(4,128)(4,1)S(1)} %get-tuple-element.28) | copy-start | bytes 12292
  237.1 256.3 %copy-start.121 = (pred[8,4,128]{2,1,0:T(4,128)(4,1)}, pred[8,4,128]{2,1,0:T(4,128)(4,1)S(1)}, u32[]{:S(2)}) copy-start(pred[8,4,128]{2,1,0:T(4,128)(4,1)S(1)} %get-tuple-element.44) | copy-start | bytes 12292
  253.9 256.7 %copy-start.122 = (pred[8,4,128]{2,1,0:T(4,128)(4,1)}, pred[8,4,128]{2,1,0:T(4,128)(4,1)S(1)}, u32[]{:S(2)}) copy-start(pred[8,4,128]{2,1,0:T(4,128)(4,1)S(1)} %get-tuple-element.52) | copy-start | bytes 12292
  526.9 256.3 %copy-start.138 = (pred[8,4,128]{2,1,0:T(4,128)(4,1)}, pred[8,4,128]{2,1,0:T(4,128)(4,1)S(1)}, u32[]{:S(2)}) copy-start(pred[8,4,128]{2,1,0:T(4,128)(4,1)S(1)} %get-tuple-element.164) | copy-start | bytes 12292
  542.9 258.1 %copy-start.139 = (pred[8,4,128]{2,1,0:T(4,128)(4,1)}, pred[8,4,128]{2,1,0:T(4,128)(4,1)S(1)}, u32[]{:S(2)}) copy-start(pred[8,4,128]{2,1,0:T(4,128)(4,1)S(1)} %get-tuple-element.172) | copy-start | bytes 12292
  542.9 258.1 %copy-start.170 = (s32[8,2]{0,1:T(2,128)S(1)}, s32[8,2]{0,1:T(2,128)}, u32[]{:S(2)}) copy-start(s32[8,2]{0,1:T(2,128)} %get-tuple-element.3255) | copy-start | bytes 196
  559.1 259.9 %copy-start.140 = (pred[8,4,128]{2,1,0:T(4,128)(4,1)}, pred[8,4,128]{2,1,0:T(4,128)(4,1)S(1)}, u32[]{:S(2)}) copy-start(pred[8,4,128]{2,1,0:T(4,128)(4,1)S(1)} %get-tuple-element.180) | copy-start | bytes 12292
  559.1 259.9 %copy-start.169 = (s32[8,2]{0,1:T(2,128)S(1)}, s32[8,2]{0,1:T(2,128)}, u32[]{:S(2)}) copy-start(s32[8,2]{0,1:T(2,128)} %get-tuple-element.3270) | copy-start | bytes 196
  576.0 260.1 %copy-start.141 = (pred[8,4,128]{2,1,0:T(4,128)(4,1)}, pred[8,4,128]{2,1,0:T(4,128)(4,1)S(1)}, u32[]{:S(2)}) copy-start(pred[8,4,128]{2,1,0:T(4,128)(4,1)S(1)} %get-tuple-element.188) | copy-start | bytes 12292
  592.9 260.2 %copy-start.142 = (pred[8,4,128]{2,1,0:T(4,128)(4,1)}, pred[8,4,128]{2,1,0:T(4,128)(4,1)S(1)}, u32[]{:S(2)}) copy-start(pred[8,4,128]{2,1,0:T(4,128)(4,1)S(1)} %get-tuple-element.196) | copy-start | bytes 12292
  610.4 260.0 %copy-start.143 = (pred[8,4,128]{2,1,0:T(4,128)(4,1)}, pred[8,4,128]{2,1,0:T(4,128)(4,1)S(1)}, u32[]{:S(2)}) copy-start(pred[8,4,128]{2,1,0:T(4,128)(4,1)S(1)} %get-tuple-element.204) | copy-start | bytes 12292
  627.9 259.3 %copy-start.144 = (pred[8,4,128]{2,1,0:T(4,128)(4,1)}, pred[8,4,128]{2,1,0:T(4,128)(4,1)S(1)}, u32[]{:S(2)}) copy-start(pred[8,4,128]{2,1,0:T(4,128)(4,1)S(1)} %get-tuple-element.372) | copy-start | bytes 12292
  643.6 261.2 %copy-start.145 = (pred[8,4,128]{2,1,0:T(4,128)(4,1)}, pred[8,4,128]{2,1,0:T(4,128)(4,1)S(1)}, u32[]{:S(2)}) copy-start(pred[8,4,128]{2,1,0:T(4,128)(4,1)S(1)} %get-tuple-element.212) | copy-start | bytes 12292
  660.7 260.7 %copy-start.146 = (pred[8,4,128]{2,1,0:T(4,128)(4,1)}, pred[8,4,128]{2,1,0:T(4,128)(4,1)S(1)}, u32[]{:S(2)}) copy-start(pred[8,4,128]{2,1,0:T(4,128)(4,1)S(1)} %get-tuple-element.220) | copy-start | bytes 12292
  660.7 260.8 %copy-start.186 = (s32[8,1]{0,1:T(1,128)S(1)}, s32[8,1]{0,1:T(1,128)}, u32[]{:S(2)}) copy-start(s32[8,1]{0,1:T(1,128)} %copy-done.185) | copy-start | bytes 100
  660.7 260.8 %copy-start.188 = (s32[8,1]{0,1:T(1,128)S(1)}, s32[8,1]{0,1:T(1,128)}, u32[]{:S(2)}) copy-start(s32[8,1]{0,1:T(1,128)} %copy-done.187) | copy-start | bytes 100
  660.7 260.8 %copy-start.190 = (s32[8,1]{0,1:T(1,128)S(1)}, s32[8,1]{0,1:T(1,128)}, u32[]{:S(2)}) copy-start(s32[8,1]{0,1:T(1,128)} %copy-done.189) | copy-start | bytes 100
  660.7 260.8 %copy-start.192 = (s32[8,1]{0,1:T(1,128)S(1)}, s32[8,1]{0,1:T(1,128)}, u32[]{:S(2)}) copy-start(s32[8,1]{0,1:T(1,128)} %copy-done.191) | copy-start | bytes 100
  660.7 260.8 %copy-start.194 = (s32[8,1]{0,1:T(1,128)S(1)}, s32[8,1]{0,1:T(1,128)}, u32[]{:S(2)}) copy-start(s32[8,1]{0,1:T(1,128)} %copy-done.193) | copy-start | bytes 100
  660.7 260.8 %copy-start.196 = (s32[8,1]{0,1:T(1,128)S(1)}, s32[8,1]{0,1:T(1,128)}, u32[]{:S(2)}) copy-start(s32[8,1]{0,1:T(1,128)} %copy-done.195) | copy-start | bytes 100
  660.7 260.8 %copy-start.198 = (s32[8,1]{0,1:T(1,128)S(1)}, s32[8,1]{0,1:T(1,128)}, u32[]{:S(2)}) copy-start(s32[8,1]{0,1:T(1,128)} %copy-done.197) | copy-start | bytes 100
  660.7 260.8 %copy-start.201 = (s32[8,1]{0,1:T(1,128)S(1)}, s32[8,1]{0,1:T(1,128)}, u32[]{:S(2)}) copy-start(s32[8,1]{0,1:T(1,128)} %copy-done.200) | copy-start | bytes 100
  660.7 260.8 %copy-start.202 = (s32[8,1]{0,1:T(1,128)S(1)}, s32[8,1]{0,1:T(1,128)}, u32[]{:S(2)}) copy-start(s32[8,1]{0,1:T(1,128)} %get-tuple-element.864) | copy-start | bytes 100
  660.7 260.8 %copy-start.203 = (s32[8,1]{0,1:T(1,128)S(1)}, s32[8,1]{0,1:T(1,128)}, u32[]{:S(2)}) copy-start(s32[8,1]{0,1:T(1,128)} %get-tuple-element.1040) | copy-start | bytes 100
  660.8 260.8 %copy-start.204 = (s32[8,1]{0,1:T(1,128)S(1)}, s32[8,1]{0,1:T(1,128)}, u32[]{:S(2)}) copy-start(s32[8,1]{0,1:T(1,128)} %get-tuple-element.1043) | copy-start | bytes 100
  660.8 260.8 %copy-start.205 = (s32[8,1]{0,1:T(1,128)S(1)}, s32[8,1]{0,1:T(1,128)}, u32[]{:S(2)}) copy-start(s32[8,1]{0,1:T(1,128)} %get-tuple-element.1046) | copy-start | bytes 100
  660.8 260.8 %copy-start.206 = (s32[8,1]{0,1:T(1,128)S(1)}, s32[8,1]{0,1:T(1,128)}, u32[]{:S(2)}) copy-start(s32[8,1]{0,1:T(1,128)} %get-tuple-element.1055) | copy-start | bytes 100
  922.4 260.9 %copy-start.28 = (s32[8]{0:T(128)}, s32[8]{0:T(128)S(1)}, u32[]{:S(2)}) copy-start(s32[8]{0:T(128)S(1)} %get-tuple-element.1190) | copy-start | bytes 100
  2013.2 6.5 collective-permute-start.3
  2015.5 4.9 collective-permute-start.2
  2020.5 5.5 collective-permute-start.5
  2021.8 4.9 collective-permute-start.4
  2032.9 8.2 collective-permute-start.6
  2039.2 7.2 collective-permute-start.7
  2046.4 5.3 collective-permute-start.9
  2047.7 4.9 collective-permute-start.8
  2083.4 6.2 collective-permute-start.10
  2086.3 8.6 collective-permute-start.11
  2095.0 5.3 collective-permute-start.13
  2096.3 5.0 collective-permute-start.12
  2152.8 7.5 collective-permute-start.14
  2156.9 11.5 collective-permute-start.15
  2170.2 5.3 collective-permute-start.17
  2171.5 5.2 collective-permute-start.16
  2247.1 10.4 collective-permute-start.19
  2249.3 9.3 collective-permute-start.18
  2258.6 5.3 collective-permute-start.21
  2259.9 4.8 collective-permute-start.20
  (171 other events, 13778.8 us)
where the time goes:
time: 2400 us; the launch traced here: 2370 us
  local copies, waits for them, and re-layouts  1870 us (78%)
  other arithmetic  254 us (11%)
  matrix products  154 us (6%)
  starting transfers between devices  67.4 us (3%)
    gather x1176, local copies, waits for them, and re-layouts  832 us
    gather x49, local copies, waits for them, and re-layouts, attend_head(): lax.dynamic_slice(key_head, (anchor, row_start, col_start), (head_dim, ro...  240 us
    gather x49, local copies, waits for them, and re-layouts, attend_head(): lax.dynamic_slice(value_head, (anchor, row_start, col_start), (head_dim,...  229 us
    mul x83, local copies, waits for them, and re-layouts, attend_head(): weights[slot_index].astype(jnp.float32) * value_block.astype(jnp.float32)  175 us
    mul x37, other arithmetic, attend_head(): weights[slot_index].astype(jnp.float32) * value_block.astype(jnp.float32)  113 us
    conv_general_dilated x1, matrix products, conv_final(): lax.conv_general_dilated(padded[None], weight, (1, 1), 'VALID', dimension...  95.1 us
    select_n x49, local copies, waits for them, and re-layouts, attend_head(): jnp.where(inside, scale_head * jnp.sum(query_head * key_block, axis=0), -...  80.2 us
    reduce_sum x49, local copies, waits for them, and re-layouts, attend_head(): jnp.sum(query_head * key_block, axis=0)  77.1 us
  transfers between devices with their start and end apart: 22, of which 12 were waited for; matrix products, arithmetic and copies ran while one was open for 38% of the time, Pallas kernels for 0%

commit v1 on v0

v1 whole, which is shorter than its diff:
```python
import functools
import math

import jax
import jax.numpy as jnp
from jax import lax
from jax.experimental import pallas as pl
from jax.experimental.pallas import tpu as pltpu
from jax.sharding import PartitionSpec as P

WIN = 7
REACH = (WIN - 1) // 2
MARGIN = REACH + 1
HALO = 2


plan_now = 0.3
plan_next = 0.5
keep_factor = math.sqrt(plan_next / plan_now)
noise_factor = math.sqrt(1.0 - plan_next) - keep_factor * math.sqrt(1.0 - plan_now)


def neighbour_rows(cells, width, dim):
    count = lax.axis_size("wide")
    head = lax.slice_in_dim(cells, 0, width, axis=dim)
    tail = lax.slice_in_dim(cells, cells.shape[dim] - width, cells.shape[dim], axis=dim)
    above = lax.ppermute(tail, "wide", [(i, i + 1) for i in range(count - 1)])
    below = lax.ppermute(head, "wide", [(i + 1, i) for i in range(count - 1)])
    return jnp.concatenate([above, cells, below], axis=dim)


def attend_kernel(
    row_count,
    col_count,
    head_dim,
    group,
    shift_ref,
    scale_ref,
    band_ref,
    query_ref,
    key_ref,
    value_ref,
    out_ref,
    query_split,
    key_split,
):
    step = pl.program_id(0)
    span = WIN * col_count
    col_step = lax.broadcasted_iota(jnp.int32, (col_count, col_count), 1) - lax.broadcasted_iota(
        jnp.int32, (col_count, col_count), 0
    )

    def unit(x):
        return x * lax.rsqrt(jnp.sum(x * x, axis=1, keepdims=True) + 1e-06)

    def halves(x):
        high = x.astype(jnp.bfloat16)
        return high, (x - high.astype(jnp.float32)).astype(jnp.bfloat16)

    for slot in range(group):
        head = step * group + slot
        lanes = slice(slot * head_dim, (slot + 1) * head_dim)
        shift_row = shift_ref[head, 0]
        shift_col = shift_ref[head, 1]
        q_high, q_low = halves(unit(query_ref[:, lanes]) * scale_ref[head])
        k_high, k_low = halves(unit(key_ref[:, lanes]))
        query_split[...] = jnp.concatenate([q_high, q_low, q_high, q_low], axis=1)
        key_split[...] = jnp.concatenate([k_high, k_high, k_low, k_low], axis=1)
        offset = col_step - shift_col
        col_bias = jnp.where((offset >= -REACH) & (offset <= REACH), 0.0, -1e30)
        for row in range(row_count):
            start = pl.multiple_of((row + shift_row + (MARGIN - REACH)) * col_count, col_count)
            scores = lax.dot_general(
                query_split[row * col_count : (row + 1) * col_count, :],
                key_split[pl.ds(start, span), :],
                (((1,), (1,)), ((), ())),
                preferred_element_type=jnp.float32,
            )
            first = band_ref[0] + row + shift_row - REACH
            pieces = []
            for k in range(WIN):
                inside = (first + k >= 0) & (first + k < band_ref[1])
                pieces.append(
                    scores[:, k * col_count : (k + 1) * col_count]
                    + (col_bias + jnp.where(inside, 0.0, -1e30))
                )
            peak = jnp.max(functools.reduce(jnp.maximum, pieces), axis=1, keepdims=True)
            pieces = [jnp.exp(piece - peak) for piece in pieces]
            total = jnp.sum(functools.reduce(jnp.add, pieces), axis=1, keepdims=True)
            norm = 1.0 / total
            weights = jnp.concatenate(
                [(piece * norm).astype(jnp.bfloat16) for piece in pieces], axis=1
            )
            mixed = jnp.dot(
                weights, value_ref[pl.ds(start, span), lanes], preferred_element_type=jnp.float32
            )
            out_ref[row * col_count : (row + 1) * col_count, lanes] = mixed.astype(jnp.bfloat16)


def window_attend(query, key, value, shifts, scales, band, row_count, col_count, head_dim):
    heads_here = shifts.shape[0]
    group = 2 if heads_here % 2 == 0 else 1
    width = group * head_dim
    cells = row_count * col_count
    cells_ext = key.shape[0]
    smem = pl.BlockSpec(memory_space=pltpu.SMEM)
    return pl.pallas_call(
        functools.partial(attend_kernel, row_count, col_count, head_dim, group),
        out_shape=jax.ShapeDtypeStruct((cells, heads_here * head_dim), jnp.bfloat16),
        grid=(heads_here // group,),
        in_specs=[
            smem,
            smem,
            smem,
            pl.BlockSpec((cells, width), lambda i: (0, i)),
            pl.BlockSpec((cells_ext, width), lambda i: (0, i)),
            pl.BlockSpec((cells_ext, width), lambda i: (0, i)),
        ],
        out_specs=pl.BlockSpec((cells, width), lambda i: (0, i)),
        scratch_shapes=[
            pltpu.VMEM((cells, 4 * head_dim), jnp.bfloat16),
            pltpu.VMEM((cells_ext, 4 * head_dim), jnp.bfloat16),
        ],
        name="window_attend",
    )(shifts, scales, band, query, key, value)


def corner_weight(weight):
    full = weight.astype(jnp.float32)
    rows = jnp.stack(
        [jnp.stack([full[0] + full[1], full[0]]), jnp.stack([full[2], full[1] + full[2]])]
    )
    left = jnp.stack([rows[:, :, 0] + rows[:, :, 1], rows[:, :, 0]], axis=2)
    right = jnp.stack([rows[:, :, 2], rows[:, :, 1] + rows[:, :, 2]], axis=2)
    taps = jnp.stack([left, right], axis=2)
    taps = jnp.transpose(taps, (0, 2, 4, 1, 3, 5)).astype(jnp.bfloat16)
    return taps.reshape(2, 2, weight.shape[2], 4 * weight.shape[3])


def conv_valid(padded, weight):
    return lax.conv_general_dilated(
        padded[None],
        weight,
        (1, 1),
        "VALID",
        dimension_numbers=("NHWC", "HWIO", "NHWC"),
        preferred_element_type=jnp.float32,
    )[0]


def inside_mask(rows, cols, row_first, col_first, row_total, col_total):
    row_index = row_first + jnp.arange(rows, dtype=jnp.int32)
    col_index = col_first + jnp.arange(cols, dtype=jnp.int32)
    row_in = (row_index >= 0) & (row_index < row_total)
    col_in = (col_index >= 0) & (col_index < col_total)
    return (row_in[:, None] & col_in[None, :])[:, :, None]


def grow(field_in, weight):
    out = jax.nn.silu(conv_valid(field_in, weight)).astype(jnp.bfloat16)
    rows, cols, channels = out.shape
    channels = channels // 4
    out = out.reshape(rows, cols, 2, 2, channels).transpose(0, 2, 1, 3, 4)
    return out.reshape(2 * rows, 2 * cols, channels)


def conv_final(padded, weight):
    rows, cols = padded.shape[0] - 2, padded.shape[1] - 2
    out_vars = weight.shape[3]
    taps = jnp.transpose(weight, (0, 1, 3, 2)).reshape(9 * out_vars, weight.shape[2])
    parts = jnp.einsum("kd,rcd->krc", taps, padded, preferred_element_type=jnp.float32)
    parts = parts.reshape(3, 3, out_vars, rows + 2, cols + 2)
    image = jnp.zeros((out_vars, rows, cols), jnp.float32)
    for a in range(3):
        for b in range(3):
            image = image + parts[a, b, :, a : a + rows, b : b + cols]
    return image


def noise_everywhere(part):
    wide = lax.axis_size("wide")
    narrow = lax.axis_size("narrow")
    rows = part.shape[1]
    pieces = {
        1: lax.slice_in_dim(part, rows - HALO, rows, axis=1),
        0: part,
        -1: lax.slice_in_dim(part, 0, HALO, axis=1),
    }
    sums = {}
    for move in (0, 1, -1):
        total = part if move == 0 else None
        for turn in range(narrow):
            if move == 0 and turn == 0:
                continue
            pairs = [
                (w * narrow + n, (w + move) * narrow + (n + turn) % narrow)
                for w in range(wide)
                for n in range(narrow)
                if 0 <= w + move < wide
            ]
            arrived = lax.ppermute(pieces[move], ("wide", "narrow"), pairs)
            total = arrived if total is None else total + arrived
        sums[move] = total
    return jnp.concatenate([sums[1], sums[0], sums[-1]], axis=1)


def shards(
    latent,
    land_sea,
    head_shift,
    logit_scale,
    embed_weight,
    land_vector,
    qkv_weight,
    out_weight,
    proj_weight,
    conv_in_weight,
    level_one_weight,
    level_two_weight,
    level_three_weight,
    conv_out_weight,
):
    channels, row_count, col_count = latent.shape
    heads_here = head_shift.shape[0]
    head_dim = qkv_weight.shape[2] // heads_here
    cells = row_count * col_count
    band_start = lax.axis_index("wide") * row_count
    total_rows = row_count * lax.axis_size("wide")

    fields = jnp.concatenate([latent, land_sea.astype(jnp.bfloat16)[None]], axis=0)
    fields = neighbour_rows(fields, MARGIN, 1)
    field_weight = jnp.concatenate([embed_weight, land_vector[None]], axis=0)
    rows_ext = row_count + 2 * MARGIN
    embedded = jnp.einsum(
        "cm,cd->md",
        fields.reshape(channels + 1, rows_ext * col_count),
        field_weight,
        preferred_element_type=jnp.float32,
    ).astype(jnp.bfloat16)
    own = lax.slice_in_dim(embedded, MARGIN * col_count, MARGIN * col_count + cells, axis=0)
    query = jnp.dot(own, qkv_weight[:, 0], preferred_element_type=jnp.float32)
    key = jnp.dot(embedded, qkv_weight[:, 1], preferred_element_type=jnp.float32)
    value = jnp.dot(embedded, qkv_weight[:, 2], preferred_element_type=jnp.float32).astype(
        jnp.bfloat16
    )
    band = jnp.stack([band_start, jnp.int32(total_rows)]).astype(jnp.int32)
    heads_out = window_attend(
        query, key, value, head_shift, logit_scale, band, row_count, col_count, head_dim
    )
    out_proj = jnp.dot(out_weight, proj_weight, preferred_element_type=jnp.float32)
    noise_part = jnp.einsum(
        "mc,rm->cr",
        out_proj,
        heads_out.astype(jnp.float32),
        precision=lax.Precision.HIGHEST,
    ).reshape(channels, row_count, col_count)
    noise = noise_everywhere(noise_part)
    near = slice((MARGIN - HALO) * col_count, (MARGIN + row_count + HALO) * col_count)
    noise = noise + jnp.einsum(
        "dc,rd->cr", proj_weight, embedded[near], preferred_element_type=jnp.float32
    ).reshape(channels, row_count + 2 * HALO, col_count)
    latent_near = fields[:channels, MARGIN - HALO : MARGIN + row_count + HALO]
    stepped = (keep_factor * latent_near.astype(jnp.float32) + noise_factor * noise).astype(
        jnp.bfloat16
    )
    tile_cols = col_count // lax.axis_size("narrow")
    col_start = lax.axis_index("narrow") * tile_cols
    stepped = jnp.pad(stepped, ((0, 0), (0, 0), (HALO, HALO)))
    stepped = lax.dynamic_slice_in_dim(stepped, col_start, tile_cols + 2 * HALO, 2)

    hidden = jax.nn.silu(conv_valid(jnp.transpose(stepped, (1, 2, 0)), conv_in_weight))
    hidden = hidden.astype(jnp.bfloat16)
    scale = 1
    for weight in (None, level_one_weight, level_two_weight, level_three_weight):
        if weight is not None:
            hidden = grow(hidden, corner_weight(weight))
            scale = 2 * scale
        mask = inside_mask(
            hidden.shape[0],
            hidden.shape[1],
            band_start * scale - 1,
            col_start * scale - 1,
            total_rows * scale,
            col_count * scale,
        )
        hidden = jnp.where(mask, hidden, jnp.zeros_like(hidden))
    return conv_final(hidden, conv_out_weight)


def solution(mesh):
    in_specs = (
        P(None, "wide", None),
        P("wide", None),
        P("narrow", None),
        P("narrow"),
        P(),
        P(),
        P(None, None, "narrow"),
        P("narrow", None),
        P(),
        P(),
        P(),
        P(),
        P(),
        P(),
    )
    out_specs = P(None, "wide", "narrow")
    return jax.shard_map(shards, mesh=mesh, in_specs=in_specs, out_specs=out_specs, check_vma=False)
```

time: 2400 us -> 324 us (0.14); the launches traced: 2370 us -> 319 us
  local copies, waits for them, and re-layouts: 1870 us -> 163 us
  other arithmetic: 254 us -> 71.1 us
  matrix products: 154 us -> 39.3 us
  starting transfers between devices: 67.4 us -> 18.9 us
  Pallas kernels: 0 us -> 24.2 us
    gather x1323 -> x0, local copies, waits for them, and re-layouts: 1340 us -> none
    mul x84 -> x0, local copies, waits for them, and re-layouts: 176 us -> none  [the longest x83 175 us: attend_head(): weights[slot_index].astype(jnp.float32) * value_block.astype(jnp.float32)]
    mul x38 -> x0, other arithmetic: 115 us -> none  [the longest x37 113 us: attend_head(): weights[slot_index].astype(jnp.float32) * value_block.astype(jnp.float32)]
    conv_general_dilated x1 -> x0, matrix products: 95.1 us -> none  [conv_final(): lax.conv_general_dilated(padded[None], weight, (1, 1), 'VALID', dimension...]
    reduce_sum x49 -> x0, local copies, waits for them, and re-layouts: 77.1 us -> none  [attend_head(): jnp.sum(query_head * key_block, axis=0)]
    select_n x49 -> x5, local copies, waits for them, and re-layouts: 80.2 us -> 19.1 us  [shards(): hidden = jnp.where(mask, hidden, jnp.zeros_like(hidden))]
    reduce_sum x6 -> x0, other arithmetic: 59.5 us -> none  [the longest x3 59.2 us: attend_head(): jnp.sum(query_head * key_block, axis=0)]
    ppermute x22 -> x7, starting transfers between devices: 67.4 us -> 18.9 us  [the longest x5 13.3 us: noise_everywhere(): arrived = lax.ppermute(pieces[move], ('wide', 'narrow'), pairs)]
  transfers between devices with their start and end apart: 22 -> 7, of which waited for: 12 -> 1; matrix products, arithmetic and copies ran while one was open for 38% -> 29% of each run, Pallas kernels for 0% -> 0%
where the time goes in v1:
time: 324 us; the launch traced here: 319 us
  local copies, waits for them, and re-layouts  163 us (50%)
  other arithmetic  71.1 us (22%)
  matrix products  39.3 us (12%)
  Pallas kernels  24.2 us (7%)
  starting transfers between devices  18.9 us (6%)
    conv_general_dilated x16, local copies, waits for them, and re-layouts, conv_valid(): lax.conv_general_dilated(padded[None], weight, (1, 1), 'VALID', dimension...  52.7 us
    convert_element_type x3, local copies, waits for them, and re-layouts, corner_weight(): taps = jnp.transpose(taps, (0, 2, 4, 1, 3, 5)).astype(jnp.bfloat16)  26 us
    pallas_call x1, Pallas kernels, window_attend(): pl.pallas_call(functools.partial(attend_kernel, row_count, col_count, hea...  24.2 us
    squeeze x3, local copies, waits for them, and re-layouts, conv_valid(): lax.conv_general_dilated(padded[None], weight, (1, 1), 'VALID', dimension...  24 us
    reshape x3, local copies, waits for them, and re-layouts, corner_weight(): return taps.reshape(2, 2, weight.shape[2], 4 * weight.shape[3])  23.6 us
    conv_general_dilated x4, matrix products, conv_valid(): lax.conv_general_dilated(padded[None], weight, (1, 1), 'VALID', dimension...  20.6 us
    select_n x5, local copies, waits for them, and re-layouts, shards(): hidden = jnp.where(mask, hidden, jnp.zeros_like(hidden))  19.1 us
    select_n x4, other arithmetic, shards(): hidden = jnp.where(mask, hidden, jnp.zeros_like(hidden))  16.9 us
  transfers between devices with their start and end apart: 7, of which 1 were waited for; matrix products, arithmetic and copies ran while one was open for 29% of the time, Pallas kernels for 0%

profile of v1, /device:TPU:21, one launch (start us, length us, event | category | flops | bytes accessed | tf_op | source)
XLA Modules:
  0.0 318.9 jit_solution(3544704420609595553)
XLA Ops:
  0.8 1.3 pad_maximum_fusion.4
  2.1 3.7 %collective-permute-start = (bf16[17,4,128]{2,1,0:T(4,128)(2,1)}, bf16[17,4,128]{2,1,0:T(4,128)(2,1)}, u32[]{:S(2)}, u32[]{:S(2)}) collective-permute-start(bf16[17,4,128]{2,1,0:T(4,128)(2,1)} %pad_maximum_fusion.4), channel_id=1, source_target_pairs={{0,2},{2,4},{4,6},{6,8},{8,10},{10,12},{12,14},{14,16},{16,18},{18... | collective-permute-start | bytes 52232 | tf_op jit(solution)/shard_map/ppermute | solution.py:27
  5.8 1.9 collective-permute-start.1
  7.8 3.8 %convert_element_type.61 = f32[3,3,512,512]{3,2,1,0:T(8,128)S(1)} convert(bf16[3,3,512,512]{3,2,1,0:T(8,128)(2,1)} %param.24) | non-fusion elementwise | flops 2359296 | bytes 14155776 | tf_op jit(solution)/shard_map/convert_element_type | solution.py:129
  12.4 1.8 slice_add_fusion.1
  14.2 1.6 maximum_bitcast_fusion.1
  15.9 2.3 fusion.87
  18.2 3.2 add_convert_fusion.1
  22.9 1.4 fusion.85
  24.2 1.6 add_convert_fusion.3
  28.7 2.8 maximum_bitcast_fusion.3
  32.2 2.4 maximum_bitcast_fusion.4
  34.6 6.2 %maximum_bitcast_fusion = bf16[2,2,512,2,2,512]{5,2,4,3,0,1:T(8,128)(2,1)} fusion(bf16[2,2,1,2,512,512]{5,4,3,1,0,2:T(8,128)(2,1)} %maximum_bitcast_fusion.4, bf16[2,2,1,2,512,512]{5,4,3,1,0,2:T(8,128)(2,1)S(1)} %maximum_bitcast_fusion.3), kind=kLoop, calls=%fused_computation.7 | loop fusion | flops 4194304 | bytes 16777216 | tf_op jit(solution)/shard_map/convert_element_type | solution.py:136
  40.9 1.8 maximum_bitcast_fusion.8
  43.0 2.3 maximum_bitcast_fusion.5
  45.7 3.4 %broadcast_and_fusion = pred[17,2,257,2]{3,1,2,0:T(4,128)(4,1)} fusion(pred[257,2]{1,0:T(8,128)(4,1)S(1)} %copy.128, pred[17,2]{1,0:T(8,128)(4,1)S(1)} %fusion.67), kind=kLoop, calls=%fused_computation.19 | loop fusion | flops 17476 | bytes 18024 | tf_op jit(solution)/shard_map/and | solution.py:156
  50.4 16.5 %copy.136 = bf16[2,2,512,2,2,512]{5,4,3,2,1,0:T(2,128)(2,1)} copy(bf16[2,2,512,2,2,512]{5,2,4,3,0,1:T(8,128)(2,1)} %maximum_bitcast_fusion) | data formatting | bytes 16777216 | tf_op jit(solution)/shard_map/convert_element_type | solution.py:136
  66.9 14.6 %reshape.235 = bf16[2,2,512,2048]{3,2,1,0:T(8,128)(2,1)} reshape(bf16[2,2,512,2,2,512]{5,4,3,2,1,0:T(2,128)(2,1)} %copy.136) | data formatting | bytes 16777216 | tf_op jit(solution)/shard_map/reshape | solution.py:137
  81.6 8.4 %copy.141 = bf16[2,2,512,2,2,256]{5,4,3,2,1,0:T(2,128)(2,1)} copy(bf16[2,2,512,2,2,256]{5,2,4,3,0,1:T(8,128)(2,1)} %maximum_bitcast_fusion.5) | data formatting | bytes 8388608 | tf_op jit(solution)/shard_map/convert_element_type | solution.py:136
  90.0 7.8 %reshape.237 = bf16[2,2,512,1024]{3,2,1,0:T(8,128)(2,1)} reshape(bf16[2,2,512,2,2,256]{5,4,3,2,1,0:T(2,128)(2,1)} %copy.141) | data formatting | bytes 8388608 | tf_op jit(solution)/shard_map/reshape | solution.py:137
  97.8 1.1 copy.146
  98.9 1.2 reshape.239
  100.1 0.9 pad_maximum_fusion.3
  101.1 1.0 convolution_convert_fusion
  102.2 3.5 %fusion.32.key_ref = f32[1536,512]{1,0:T(8,128)} fusion(bf16[1536,1024]{1,0:T(8,128)(2,1)S(1)} %convolution_convert_fusion, bf16[1024,3,512]{2,0,1:T(8,128)(2,1)S(1)} %copy-done.20), kind=kOutput, calls=%fused_computation.77 | convolution fusion | flops 1610612736 | bytes 7340032 | tf_op jit(solution)/shard_map/dot_general | solution.py:242
  105.6 3.0 convolution_convert_fusion.1.value_ref
  108.6 1.8 fusion.29.query_ref
  110.4 24.2 %window_attend.1 = bf16[512,512]{1,0:T(8,128)(2,1)} custom-call(s32[8,2]{1,0:T(8,128)} %copy.129.shift_ref, f32[8]{0:T(128)} %scale_ref.1, s32[2]{0:T(128)} %pad_add_fusion.band_ref, f32[512,512]{1,0:T(8,128)} %fusion.29.query_ref, f32[1536,512]{1,0:T(8,128)} %fusion.32.key_ref, bf16[1536,512]{1,0:T(8,128)(2,1)} %convolution_convert_fusion.1.value_ref), custom_call_target="tpu_custom_call" | custom-call | tf_op jit(solution)/shard_map/window_attend/pallas_call | solution.py:107
  134.5 1.6 fusion.95
  136.2 4.5 %collective-permute-start.2 = (f32[16,2,128]{2,1,0:T(2,128)S(1)}, f32[16,2,128]{2,1,0:T(2,128)S(1)}, u32[]{:S(2)}, u32[]{:S(2)}) collective-permute-start(f32[16,2,128]{2,1,0:T(2,128)S(1)} %get-tuple-element.29), channel_id=1, source_target_pairs={{0,2},{1,3},{2,4},{3,5},{4,6},{5,7},{6,8},{7,9},{8,10},{9,11},{10,... | collective-permute-start | bytes 49160 | tf_op jit(solution)/shard_map/ppermute | solution.py:201
  140.7 2.9 collective-permute-start.3
  143.6 2.6 collective-permute-start.5
  146.2 2.1 collective-permute-start.6
  148.2 1.3 collective-permute-start.4
  149.5 2.2 fusion.26
  151.8 1.2 collective-permute-done.6
  153.5 1.1 multiply_convert_fusion
  155.3 5.8 %convolution_select_fusion = f32[5,8,9,2048]{3,1,2,0:T(8,128)S(1)} fusion(bf16[2,2,512,2048]{3,2,1,0:T(8,128)(2,1)} %reshape.235, pred[8,9]{0,1:T(8,128)(4,1)S(1)} %copy-done.24, bf16[6,1,7,1,512]{4,2,3,0,1:T(8,128)(2,1)S(1)} %slice.173, bf16[6,1,8,9,512]{4,2,3,0,1:T(8,128)(2,1)S(1)} %copy.135), kind=kOutput, calls=%fused_computation.36 | convolution fusion | flops 3022110720 | bytes 11823176 | tf_op jit(solution)/shard_map/conv_general_dilated | solution.py:141
  161.1 4.2 %copy.137 = f32[5,8,9,2048]{3,2,1,0:T(8,128)} copy(f32[5,8,9,2048]{3,1,2,0:T(8,128)S(1)} %convolution_select_fusion) | data formatting | bytes 5898240 | tf_op jit(solution)/shard_map/conv_general_dilated | solution.py:141
  165.2 4.8 %reshape.255 = f32[5,1,72,2048]{3,2,0,1:T(8,128)} reshape(f32[5,8,9,2048]{3,2,1,0:T(8,128)} %copy.137) | data formatting | bytes 5898240 | tf_op jit(solution)/shard_map/conv_general_dilated | solution.py:141
  170.0 4.9 %squeeze.23 = f32[5,65,2,2,512]{4,3,2,1,0:T(2,128)} reshape(f32[5,1,65,2048]{3,2,0,1:T(8,128)} %bitcast.124) | data formatting | bytes 5324800 | tf_op jit(solution)/shard_map/squeeze | solution.py:141
  174.9 4.2 %fusion.24 = bf16[5,2,65,2,512]{4,3,1,2,0:T(2,128)(2,1)S(1)} fusion(f32[5,65,2,2,512]{4,3,2,1,0:T(2,128)} %squeeze.23), kind=kLoop, calls=%fused_computation.69 | loop fusion | flops 3328000 | bytes 3993600 | tf_op jit(solution)/shard_map/transpose | solution.py:163
  179.2 2.0 copy.138
  181.2 3.2 %reshape.236 = bf16[1,10,130,512]{3,2,1,0:T(8,128)(2,1)S(1)} reshape(bf16[5,2,65,2,512]{4,3,2,1,0:T(2,128)(2,1)} %copy.138) | data formatting | bytes 2662400 | tf_op jit(solution)/shard_map/reshape | solution.py:164
  184.7 1.2 pad.9
  185.9 2.4 reshape.258
  188.8 8.5 %broadcast_select_fusion.2 = f32[9,8,17,1024]{3,1,2,0:T(8,128)S(1)} fusion(pred[8,17]{0,1:T(8,128)(4,1)S(1)} %copy-done.23, bf16[2,2,512,1024]{3,2,1,0:T(8,128)(2,1)} %reshape.237, bf16[10,1,7,1,512]{4,2,3,0,1:T(8,128)(2,1)S(1)} %slice.182, bf16[10,1,8,17,512]{4,2,3,0,1:T(8,128)(2,1)S(1)} %copy.140), kind=kOutput, calls=%fused_computation.44 | convolution fusion | flops 5139505152 | bytes 10672264 | tf_op jit(solution)/shard_map/conv_general_dilated | solution.py:141
  197.3 5.9 %copy.142 = f32[9,8,17,1024]{3,2,1,0:T(8,128)} copy(f32[9,8,17,1024]{3,1,2,0:T(8,128)S(1)} %broadcast_select_fusion.2) | data formatting | bytes 10027008 | tf_op jit(solution)/shard_map/conv_general_dilated | solution.py:141
  203.2 6.7 %reshape.262 = f32[9,1,136,1024]{3,2,0,1:T(8,128)} reshape(f32[9,8,17,1024]{3,2,1,0:T(8,128)} %copy.142) | data formatting | bytes 10027008 | tf_op jit(solution)/shard_map/conv_general_dilated | solution.py:141
  209.9 7.5 %squeeze.24 = f32[9,129,2,2,256]{4,3,2,1,0:T(2,128)} reshape(f32[9,1,129,1024]{3,2,0,1:T(8,128)} %bitcast.123) | data formatting | bytes 9510912 | tf_op jit(solution)/shard_map/squeeze | solution.py:141
  217.4 6.6 %fusion.13 = bf16[9,2,129,2,256]{4,3,1,2,0:T(2,128)(2,1)S(1)} fusion(f32[9,129,2,2,256]{4,3,2,1,0:T(2,128)} %squeeze.24), kind=kLoop, calls=%fused_computation.46 | loop fusion | flops 5944320 | bytes 7133184 | tf_op jit(solution)/shard_map/transpose | solution.py:163
  224.0 3.1 copy.143
  227.0 5.1 %reshape.238 = bf16[1,18,258,256]{3,2,1,0:T(8,128)(2,1)S(1)} reshape(bf16[9,2,129,2,256]{4,3,2,1,0:T(2,128)(2,1)} %copy.143) | data formatting | bytes 4755456 | tf_op jit(solution)/shard_map/reshape | solution.py:164
  233.2 2.8 reshape.265
  236.1 2.5 copy.145
  238.6 5.2 %broadcast_select_fusion.1 = f32[17,8,33,512]{3,1,2,0:T(8,128)S(1)} fusion(pred[8,33]{0,1:T(8,128)(4,1)S(1)} %copy-done.22, bf16[2,2,256,512]{3,2,1,0:T(8,128)(2,1)S(1)} %copy-done.10, bf16[18,1,7,1,256]{4,2,3,0,1:T(8,128)(2,1)S(1)} %slice.191, bf16[18,1,8,33,256]{4,2,3,0,1:T(8,128)(2,1)S(1)} %copy.145), kind=kOutput, calls=%fused_computation.18 | convolution fusion | flops 4715827200 | bytes 12737800 | tf_op jit(solution)/shard_map/conv_general_dilated | solution.py:141
  243.9 11.7 %copy.147 = f32[17,8,33,512]{3,2,1,0:T(8,128)} copy(f32[17,8,33,512]{3,1,2,0:T(8,128)S(1)} %broadcast_select_fusion.1) | data formatting | bytes 18382848 | tf_op jit(solution)/shard_map/conv_general_dilated | solution.py:141
  255.6 11.1 %reshape.269 = f32[17,1,264,512]{3,2,0,1:T(8,128)} reshape(f32[17,8,33,512]{3,2,1,0:T(8,128)} %copy.147) | data formatting | bytes 18382848 | tf_op jit(solution)/shard_map/conv_general_dilated | solution.py:141
  266.6 11.6 %squeeze.25 = f32[17,257,2,2,128]{4,3,2,1,0:T(2,128)} reshape(f32[17,1,257,512]{3,2,0,1:T(8,128)} %bitcast.122) | data formatting | bytes 17895424 | tf_op jit(solution)/shard_map/squeeze | solution.py:141
  278.3 15.6 %broadcast_select_fusion = bf16[17,2,257,2,128]{4,3,1,2,0:T(2,128)(2,1)} fusion(pred[17,2,257,2]{3,1,2,0:T(4,128)(4,1)S(1)} %copy-done.4, f32[17,257,2,2,128]{4,3,2,1,0:T(2,128)} %squeeze.25), kind=kLoop, calls=%fused_computation.6 | loop fusion | flops 13421568 | bytes 13439044 | tf_op jit(solution)/shard_map/jit(_where)/select_n | solution.py:286
  293.8 7.4 %copy.148 = bf16[17,2,257,2,128]{4,3,2,1,0:T(2,128)(2,1)} copy(bf16[17,2,257,2,128]{4,3,1,2,0:T(2,128)(2,1)} %broadcast_select_fusion) | data formatting | bytes 8947712 | tf_op jit(solution)/shard_map/jit(_where)/select_n | solution.py:286
  301.2 10.3 %select_n.42 = bf16[34,514,128]{2,1,0:T(8,128)(2,1)} reshape(bf16[17,2,257,2,128]{4,3,2,1,0:T(2,128)(2,1)} %copy.148) | data formatting | bytes 8947712 | tf_op jit(solution)/shard_map/jit(_where)/select_n | solution.py:286
  311.5 5.4 %convolution_bitcast_fusion = f32[36,34,514]{2,0,1:T(8,128)S(1)} fusion(bf16[34,514,128]{2,1,0:T(8,128)(2,1)} %select_n.42, bf16[36,128,1]{1,0,2:T(8,128)(2,1)S(1)} %reshape.299), kind=kOutput, calls=%fused_computation.56 | convolution fusion | flops 161058816 | bytes 6999616 | tf_op jit(solution)/shard_map/kd,rcd->krc/dot_general | solution.py:171
  317.5 1.2 fusion.49
  (117 shorter events, 12.2 us)
Async XLA Ops:
  0.0 28.2 %copy-start = (bf16[512,1024]{1,0:T(8,128)(2,1)S(1)}, bf16[512,1024]{1,0:T(8,128)(2,1)}, u32[]{:S(2)}) copy-start(bf16[512,1024]{1,0:T(8,128)(2,1)} %param.21) | copy-start | bytes 3145732
  2.1 98.0 %collective-permute-start = (bf16[17,4,128]{2,1,0:T(4,128)(2,1)}, bf16[17,4,128]{2,1,0:T(4,128)(2,1)}, u32[]{:S(2)}, u32[]{:S(2)}) collective-permute-start(bf16[17,4,128]{2,1,0:T(4,128)(2,1)} %pad_maximum_fusion.4), channel_id=1, source_target_pairs={{0,2},{2,4},{4,6},{6,8},{8,10},{10,12},{12,14},{14,16},{16,18},{18... | collective-permute-start | bytes 52232 | tf_op jit(solution)/shard_map/ppermute | solution.py:27
  5.8 94.3 %collective-permute-start.1 = (bf16[17,4,128]{2,1,0:T(4,128)(2,1)}, bf16[17,4,128]{2,1,0:T(4,128)(2,1)}, u32[]{:S(2)}, u32[]{:S(2)}) collective-permute-start(bf16[17,4,128]{2,1,0:T(4,128)(2,1)} %pad_maximum_fusion.4), channel_id=1, source_target_pairs={{2,0},{4,2},{6,4},{8,6},{10,8},{12,10},{14,12},{16,14},{18,16},{20... | collective-permute-start | bytes 52232 | tf_op jit(solution)/shard_map/ppermute | solution.py:28
  7.7 3.8 %copy-start.2 = (bf16[3,3,512,512]{3,2,1,0:T(8,128)(2,1)S(1)}, bf16[3,3,512,512]{3,2,1,0:T(8,128)(2,1)}, u32[]{:S(2)}) copy-start(bf16[3,3,512,512]{3,2,1,0:T(8,128)(2,1)} %param.24) | copy-start | bytes 14155780
  18.2 3.2 copy-start.3
  24.2 1.6 copy-start.8
  26.1 2.1 copy-start.16
  28.7 2.9 copy-start.5
  28.7 3.5 %copy-start.6 = (bf16[2,2,1,512,512]{4,3,2,1,0:T(8,128)(2,1)S(1)}, bf16[2,2,1,512,512]{4,3,2,1,0:T(8,128)(2,1)}, u32[]{:S(2)}) copy-start(bf16[2,2,1,512,512]{4,3,2,1,0:T(8,128)(2,1)} %get-tuple-element.6) | copy-start | bytes 6291460
  40.8 1.9 copy-start.7
  42.9 2.4 copy-start.12
  43.0 2.4 copy-start.13
  43.0 2.5 copy-start.11
  45.4 4.3 %copy-start.18 = (bf16[1024]{0:T(1024)(128)(2,1)S(1)}, bf16[1024]{0:T(1024)(128)(2,1)}, u32[]{:S(2)}) copy-start(bf16[1024]{0:T(1024)(128)(2,1)} %param.19) | copy-start | bytes 6148
  45.4 4.3 %copy-start.19 = (s32[8,2]{0,1:T(2,128)S(1)}, s32[8,2]{0,1:T(2,128)}, u32[]{:S(2)}) copy-start(s32[8,2]{0,1:T(2,128)} %param.16) | copy-start | bytes 196
  97.8 2.3 copy-start.17
  97.8 2.4 copy-start.14
  97.8 3.3 %copy-start.15 = (bf16[16,1024]{1,0:T(8,128)(2,1)S(1)}, bf16[16,1024]{1,0:T(8,128)(2,1)}, u32[]{:S(2)}) copy-start(bf16[16,1024]{1,0:T(8,128)(2,1)} %param.18) | copy-start | bytes 98308
  100.1 2.1 copy-start.20
  102.2 6.5 %copy-start.9 = (bf16[1536,1024]{1,0:T(8,128)(2,1)}, bf16[1536,1024]{1,0:T(8,128)(2,1)S(1)}, u32[]{:S(2)}) copy-start(bf16[1536,1024]{1,0:T(8,128)(2,1)S(1)} %convolution_convert_fusion) | copy-start | bytes 9437188
  134.5 19.0 %copy-start.21 = (bf16[3,3,16,512]{3,2,1,0:T(8,128)(2,1)S(1)}, bf16[3,3,16,512]{3,2,1,0:T(8,128)(2,1)}, u32[]{:S(2)}) copy-start(bf16[3,3,16,512]{3,2,1,0:T(8,128)(2,1)} %param.23) | copy-start | bytes 442372
  134.5 19.0 %copy-start.25 = (pred[8,9]{0,1:T(8,128)(4,1)S(1)}, pred[8,9]{0,1:T(8,128)(4,1)}, u32[]{:S(2)}) copy-start(pred[8,9]{0,1:T(8,128)(4,1)} %constant.104) | copy-start | bytes 220
  136.2 15.6 %collective-permute-start.2 = (f32[16,2,128]{2,1,0:T(2,128)S(1)}, f32[16,2,128]{2,1,0:T(2,128)S(1)}, u32[]{:S(2)}, u32[]{:S(2)}) collective-permute-start(f32[16,2,128]{2,1,0:T(2,128)S(1)} %get-tuple-element.29), channel_id=1, source_target_pairs={{0,2},{1,3},{2,4},{3,5},{4,6},{5,7},{6,8},{7,9},{8,10},{9,11},{10,... | collective-permute-start | bytes 49160 | tf_op jit(solution)/shard_map/ppermute | solution.py:201
  140.7 11.1 %collective-permute-start.3 = (f32[16,2,128]{2,1,0:T(2,128)S(1)}, f32[16,2,128]{2,1,0:T(2,128)S(1)}, u32[]{:S(2)}, u32[]{:S(2)}) collective-permute-start(f32[16,2,128]{2,1,0:T(2,128)S(1)} %get-tuple-element.29), channel_id=1, source_target_pairs={{0,3},{1,2},{2,5},{3,4},{4,7},{5,6},{6,9},{7,8},{8,11},{9,10},{10,... | collective-permute-start | bytes 49160 | tf_op jit(solution)/shard_map/ppermute | solution.py:201
  143.6 8.2 %collective-permute-start.5 = (f32[16,2,128]{2,1,0:T(2,128)S(1)}, f32[16,2,128]{2,1,0:T(2,128)S(1)}, u32[]{:S(2)}, u32[]{:S(2)}) collective-permute-start(f32[16,2,128]{2,1,0:T(2,128)S(1)} %get-tuple-element.30), channel_id=1, source_target_pairs={{2,0},{3,1},{4,2},{5,3},{6,4},{7,5},{8,6},{9,7},{10,8},{11,9},{12,... | collective-permute-start | bytes 49160 | tf_op jit(solution)/shard_map/ppermute | solution.py:201
  146.2 6.9 %collective-permute-start.6 = (f32[16,2,128]{2,1,0:T(2,128)S(1)}, f32[16,2,128]{2,1,0:T(2,128)S(1)}, u32[]{:S(2)}, u32[]{:S(2)}) collective-permute-start(f32[16,2,128]{2,1,0:T(2,128)S(1)} %get-tuple-element.30), channel_id=1, source_target_pairs={{2,1},{3,0},{4,3},{5,2},{6,5},{7,4},{8,7},{9,6},{10,9},{11,8},{12,... | collective-permute-start | bytes 49160 | tf_op jit(solution)/shard_map/ppermute | solution.py:201
  148.2 4.8 %collective-permute-start.4 = (f32[16,4,128]{2,1,0:T(4,128)S(1)}, f32[16,4,128]{2,1,0:T(4,128)S(1)}, u32[]{:S(2)}, u32[]{:S(2)}) collective-permute-start(f32[16,4,128]{2,1,0:T(4,128)S(1)} %reshape.233), channel_id=1, source_target_pairs={{0,1},{1,0},{2,3},{3,2},{4,5},{5,4},{6,7},{7,6},{8,9},{9,8},{10,11... | collective-permute-start | bytes 98312 | tf_op jit(solution)/shard_map/ppermute | solution.py:201
  154.6 0.7 copy-start.24
  185.9 2.9 copy-start.23
  236.0 2.6 copy-start.10
  236.0 2.6 copy-start.22
  266.6 11.6 %copy-start.4 = (pred[17,2,257,2]{3,1,2,0:T(4,128)(4,1)S(1)}, pred[17,2,257,2]{3,1,2,0:T(4,128)(4,1)}, u32[]{:S(2)}) copy-start(pred[17,2,257,2]{3,1,2,0:T(4,128)(4,1)} %broadcast_and_fusion) | copy-start | bytes 52432
  311.5 7.3 %copy-start.1 = (bf16[512,1024]{1,0:T(8,128)(2,1)S(1)}, bf16[512,1024]{1,0:T(8,128)(2,1)}, u32[]{:S(2)}) copy-start(bf16[512,1024]{1,0:T(8,128)(2,1)} %param.21) | copy-start | bytes 3145732

commit v2 on v1

--- a/solution.py
+++ b/solution.py
@@ -125,16 +125,65 @@
     )(shifts, scales, band, query, key, value)
 
 
-def corner_weight(weight):
-    full = weight.astype(jnp.float32)
-    rows = jnp.stack(
-        [jnp.stack([full[0] + full[1], full[0]]), jnp.stack([full[2], full[1] + full[2]])]
-    )
-    left = jnp.stack([rows[:, :, 0] + rows[:, :, 1], rows[:, :, 0]], axis=2)
-    right = jnp.stack([rows[:, :, 2], rows[:, :, 1] + rows[:, :, 2]], axis=2)
-    taps = jnp.stack([left, right], axis=2)
-    taps = jnp.transpose(taps, (0, 2, 4, 1, 3, 5)).astype(jnp.bfloat16)
-    return taps.reshape(2, 2, weight.shape[2], 4 * weight.shape[3])
+def grow_kernel(phases, row_total, col_total, base_ref, field_ref, turned_ref, weight_ref, out_ref, taps):
+    odd = pl.program_id(0)
+    depth, width = weight_ref.shape[2], weight_ref.shape[3]
+    rows, stride = out_ref.shape[1], out_ref.shape[3]
+    chunk = min(depth, 64)
+    first = jnp.where(odd == 0, 1.0, 0.0)
+
+    def combine(index, carry):
+        start = pl.multiple_of(index * chunk, chunk)
+        for a in range(2):
+            edge = []
+            for b in range(3):
+                middle = weight_ref[1, b, pl.ds(start, chunk), :].astype(jnp.float32)
+                outer = weight_ref[2 * a, b, pl.ds(start, chunk), :].astype(jnp.float32)
+                edge.append(outer + middle * (first if a == 0 else 1.0 - first))
+            left = jnp.concatenate([edge[0] + edge[1], edge[0]], axis=1)
+            right = jnp.concatenate([edge[2], edge[1] + edge[2]], axis=1)
+            taps[pl.ds(2 * a * depth + start, chunk), :] = left.astype(jnp.bfloat16)
+            taps[pl.ds((2 * a + 1) * depth + start, chunk), :] = right.astype(jnp.bfloat16)
+        return carry
+
+    lax.fori_loop(0, depth // chunk, combine, 0)
+    row_index = (
+        2 * lax.broadcasted_iota(jnp.int32, (rows, stride, 1), 0) + odd + base_ref[0]
+    )
+    col_step = lax.broadcasted_iota(jnp.int32, (rows, stride, 1), 1)
+    row_in = (row_index >= 0) & (row_index < row_total)
+    for p in range(phases):
+        def near(a):
+            here = field_ref[p, a : a + rows]
+            after = field_ref[p + 1, a : a + rows] if p < phases - 1 else turned_ref[a : a + rows]
+            return [piece.reshape(rows * stride, depth) for piece in (here, after)]
+
+        lhs = jnp.concatenate(near(0) + near(1), axis=1)
+        total = jnp.dot(lhs, taps[...], preferred_element_type=jnp.float32)
+        total = total.reshape(rows, stride, 2 * width)
+        for side in range(2):
+            value = total[:, :, side * width : (side + 1) * width]
+            value = value / (1.0 + jnp.exp(-value))
+            col_index = 2 * phases * col_step + (2 * p + side) + base_ref[1]
+            inside = row_in & (col_index >= 0) & (col_index < col_total)
+            out_ref[2 * p + side, :, 0] = jnp.where(inside, value, 0.0).astype(jnp.bfloat16)
+
+
+def grow(field_in, weight, base, row_total, col_total):
+    phases, rows, stride, depth = field_in.shape
+    width = weight.shape[3]
+    turned = jnp.roll(field_in[0], -1, axis=1)
+    whole = pl.BlockSpec(memory_space=pltpu.VMEM)
+    out = pl.pallas_call(
+        functools.partial(grow_kernel, phases, row_total, col_total),
+        out_shape=jax.ShapeDtypeStruct((2 * phases, rows - 1, 2, stride, width), jnp.bfloat16),
+        grid=(2,),
+        in_specs=[pl.BlockSpec(memory_space=pltpu.SMEM), whole, whole, whole],
+        out_specs=pl.BlockSpec((2 * phases, rows - 1, 1, stride, width), lambda i: (0, 0, i, 0, 0)),
+        scratch_shapes=[pltpu.VMEM((4 * depth, 2 * width), jnp.bfloat16)],
+        name="grow",
+    )(base, field_in, turned, weight)
+    return out.reshape(2 * phases, 2 * (rows - 1), stride, width)
 
 
 def conv_valid(padded, weight):
@@ -156,25 +205,32 @@
     return (row_in[:, None] & col_in[None, :])[:, :, None]
 
 
-def grow(field_in, weight):
-    out = jax.nn.silu(conv_valid(field_in, weight)).astype(jnp.bfloat16)
-    rows, cols, channels = out.shape
-    channels = channels // 4
-    out = out.reshape(rows, cols, 2, 2, channels).transpose(0, 2, 1, 3, 4)
-    return out.reshape(2 * rows, 2 * cols, channels)
-
-
-def conv_final(padded, weight):
-    rows, cols = padded.shape[0] - 2, padded.shape[1] - 2
+def conv_final(field_in, weight, rows, cols):
+    phases, rows_in, stride, depth = field_in.shape
     out_vars = weight.shape[3]
-    taps = jnp.transpose(weight, (0, 1, 3, 2)).reshape(9 * out_vars, weight.shape[2])
-    parts = jnp.einsum("kd,rcd->krc", taps, padded, preferred_element_type=jnp.float32)
-    parts = parts.reshape(3, 3, out_vars, rows + 2, cols + 2)
-    image = jnp.zeros((out_vars, rows, cols), jnp.float32)
-    for a in range(3):
-        for b in range(3):
-            image = image + parts[a, b, :, a : a + rows, b : b + cols]
-    return image
+    steps = cols // phases
+    taps = jnp.transpose(weight, (0, 1, 3, 2)).reshape(9 * out_vars, depth)
+    parts = lax.dot_general(
+        taps,
+        field_in.reshape(phases * rows_in * stride, depth),
+        (((1,), (1,)), ((), ())),
+        preferred_element_type=jnp.float32,
+    ).reshape(3, 3, out_vars, phases, rows_in, stride)
+    strips = []
+    for q in range(phases):
+        strip = jnp.zeros((out_vars, rows, steps), jnp.float32)
+        for a in range(3):
+            for b in range(3):
+                p, skip = (q + b) % phases, (q + b) // phases
+                strip = strip + parts[a, b, :, p, a : a + rows, skip : skip + steps]
+        strips.append(strip)
+    strips = jnp.concatenate(strips, axis=2)
+    source = lax.broadcasted_iota(jnp.int32, (cols, cols), 0)
+    target = lax.broadcasted_iota(jnp.int32, (cols, cols), 1)
+    order = (source % steps) * phases + source // steps == target
+    return jnp.einsum(
+        "vrs,st->vrt", strips, order.astype(jnp.float32), precision=lax.Precision.HIGHEST
+    )
 
 
 def noise_everywhere(part):
@@ -270,21 +326,18 @@
 
     hidden = jax.nn.silu(conv_valid(jnp.transpose(stepped, (1, 2, 0)), conv_in_weight))
     hidden = hidden.astype(jnp.bfloat16)
+    mask = inside_mask(
+        hidden.shape[0], hidden.shape[1], band_start - 1, col_start - 1, total_rows, col_count
+    )
+    hidden = jnp.where(mask, hidden, jnp.zeros_like(hidden))
+    spare = -hidden.shape[1] % 16
+    hidden = jnp.pad(hidden, ((0, 0), (0, spare), (0, 0)))[None]
     scale = 1
-    for weight in (None, level_one_weight, level_two_weight, level_three_weight):
-        if weight is not None:
-            hidden = grow(hidden, corner_weight(weight))
-            scale = 2 * scale
-        mask = inside_mask(
-            hidden.shape[0],
-            hidden.shape[1],
-            band_start * scale - 1,
-            col_start * scale - 1,
-            total_rows * scale,
-            col_count * scale,
-        )
-        hidden = jnp.where(mask, hidden, jnp.zeros_like(hidden))
-    return conv_final(hidden, conv_out_weight)
+    for weight in (level_one_weight, level_two_weight, level_three_weight):
+        scale = 2 * scale
+        base = jnp.stack([band_start * scale - 1, col_start * scale - 1]).astype(jnp.int32)
+        hidden = grow(hidden, weight, base, total_rows * scale, col_count * scale)
+    return conv_final(hidden, conv_out_weight, row_count * scale, tile_cols * scale)
 
 
 def solution(mesh):

time: 324 us -> 134 us (0.41); the launches traced: 319 us -> 133 us
  local copies, waits for them, and re-layouts: 163 us -> 14.8 us
  other arithmetic: 71.1 us -> 12.6 us
  Pallas kernels: 24.2 us -> 59.3 us
  matrix products: 39.3 us -> 26.3 us
    conv_general_dilated x16 -> x0, local copies, waits for them, and re-layouts: 52.7 us -> none  [conv_valid(): lax.conv_general_dilated(padded[None], weight, (1, 1), 'VALID', dimension...]
    pallas_call x0 -> x3, Pallas kernels: none -> 35.5 us  [grow(): pl.pallas_call(functools.partial(grow_kernel, phases, row_total, col_tota...]
    convert_element_type x4 -> x0, local copies, waits for them, and re-layouts: 26.2 us -> none  [the longest x3 26 us: corner_weight(): taps = jnp.transpose(taps, (0, 2, 4, 1, 3, 5)).astype(jnp.bfloat16)]
    reshape x7 -> x2, local copies, waits for them, and re-layouts: 32.6 us -> 7.55 us  [the longest x1 6.83 us: conv_final(): parts = lax.dot_general(taps, field_in.reshape(phases * rows_in * stride,...]
    squeeze x3 -> x0, local copies, waits for them, and re-layouts: 24 us -> none  [conv_valid(): lax.conv_general_dilated(padded[None], weight, (1, 1), 'VALID', dimension...]
    select_n x5 -> x0, local copies, waits for them, and re-layouts: 19.1 us -> none  [shards(): hidden = jnp.where(mask, hidden, jnp.zeros_like(hidden))]
    conv_general_dilated x4 -> x1, matrix products: 20.6 us -> 1.58 us  [conv_valid(): lax.conv_general_dilated(padded[None], weight, (1, 1), 'VALID', dimension...]
    another operation x15 -> x3, other arithmetic: 19.6 us -> 1.87 us  [shards(): jnp.stack([band_start * scale - 1, col_start * scale - 1]).astype(jnp.int32)]
  transfers between devices with their start and end apart: 7 -> 7, of which waited for: 1 -> 0; matrix products, arithmetic and copies ran while one was open for 29% -> 7% of each run, Pallas kernels for 0% -> 0%
where the time goes in v2:
time: 134 us; the launch traced here: 133 us
  Pallas kernels  59.3 us (44%)
  matrix products  26.3 us (20%)
  starting transfers between devices  19.6 us (15%)
  local copies, waits for them, and re-layouts  14.8 us (11%)
  other arithmetic  12.6 us (9%)
    pallas_call x3, Pallas kernels, grow(): pl.pallas_call(functools.partial(grow_kernel, phases, row_total, col_tota...  35.5 us
    pallas_call x1, Pallas kernels, window_attend(): pl.pallas_call(functools.partial(attend_kernel, row_count, col_count, hea...  23.8 us
    ppermute x5, starting transfers between devices, noise_everywhere(): arrived = lax.ppermute(pieces[move], ('wide', 'narrow'), pairs)  13.1 us
    dot_general x1, matrix products, conv_final(): lax.dot_general(taps, field_in.reshape(phases * rows_in * stride, depth),...  7.82 us
    reshape x1, local copies, waits for them, and re-layouts, conv_final(): parts = lax.dot_general(taps, field_in.reshape(phases * rows_in * stride,...  6.83 us
    add x4, other arithmetic, conv_final(): strip = strip + parts[a, b, :, p, a:a + rows, skip:skip + steps]  6.14 us
    ppermute x1, starting transfers between devices, neighbour_rows(): above = lax.ppermute(tail, 'wide', [(i, i + 1) for i in range(count - 1)])  3.88 us
    dot_general x1, matrix products, shards(): jnp.dot(embedded, qkv_weight[:, 1], preferred_element_type=jnp.float32)  3.49 us
  transfers between devices with their start and end apart: 7, of which 0 were waited for; matrix products, arithmetic and copies ran while one was open for 7% of the time, Pallas kernels for 0%

profile of v2, /device:TPU:21, one launch (start us, length us, event | category | flops | bytes accessed | tf_op | source)
XLA Modules:
  0.0 132.9 jit_solution(12696305314927191665)
XLA Ops:
  0.0 0.0 copy-start
  0.0 0.8 copy_dynamic-update-slice_fusion
  0.8 0.7 convert_bitcast_fusion
  1.5 2.6 %collective-permute-start.1 = (bf16[17,4,128]{2,0,1:T(8,128)(2,1)S(1)}, bf16[17,4,128]{2,0,1:T(8,128)(2,1)S(1)}, u32[]{:S(2)}, u32[]{:S(2)}) collective-permute-start(bf16[17,4,128]{2,0,1:T(8,128)(2,1)S(1)} %constant_dynamic-update-slice_fusion), channel_id=1, source_target_pairs={{2,0},{4,2},{6,4},{8,6},{10,8},{12,10},{14,12},{16,14},{18,16},{20... | collective-permute-start | bytes 52232 | tf_op jit(solution)/shard_map/ppermute | solution.py:28
  4.1 3.9 %collective-permute-start = (bf16[17,4,128]{2,0,1:T(8,128)(2,1)S(1)}, bf16[17,4,128]{2,0,1:T(8,128)(2,1)S(1)}, u32[]{:S(2)}, u32[]{:S(2)}) collective-permute-start(bf16[17,4,128]{2,0,1:T(8,128)(2,1)S(1)} %constant_dynamic-update-slice_fusion), channel_id=1, source_target_pairs={{0,2},{2,4},{4,6},{6,8},{8,10},{10,12},{12,14},{14,16},{16,18},{18... | collective-permute-start | bytes 52232 | tf_op jit(solution)/shard_map/ppermute | solution.py:27
  8.1 0.7 pad_add_fusion.base_ref
  8.7 0.6 pad_add_fusion.1.base_ref
  9.3 0.6 pad_add_fusion.2.base_ref
  9.9 0.0 copy-done
  10.0 1.1 fusion.119
  11.1 0.1 broadcast_and_fusion
  11.2 0.6 pad_add_fusion.3.band_ref
  11.8 0.7 broadcast_in_dim.28
  12.4 1.3 %copy.178.shift_ref = s32[8,2]{1,0:T(8,128)} copy(s32[8,2]{0,1:T(2,128)} %param.16) | data formatting | bytes 128 | tf_op args[2]
  13.8 0.7 reshape.103
  14.5 0.0 copy-start.3
  14.5 0.0 collective-permute-done.1
  14.5 0.0 collective-permute-done
  14.6 1.9 %convolution_convert_fusion = bf16[1536,1024]{1,0:T(8,128)(2,1)S(1)} fusion(bf16[17,1536]{1,0:T(8,128)(2,1)S(1)} %bitcast.524, bf16[1,1024]{1,0:T(2,128)(2,1)S(1)} %broadcast_in_dim.28, bf16[16,1024]{1,0:T(8,128)(2,1)} %param.18), kind=kOutput, calls=%fused_computation.1 | convolution fusion | flops 55119872 | bytes 3232768 | tf_op jit(solution)/shard_map/cm,cd->md/dot_general | solution.py:290
  16.6 0.0 copy-done.3
  16.6 0.0 copy-start.1
  16.6 2.0 %fusion.5.query_ref = f32[512,512]{1,0:T(8,128)} fusion(bf16[1536,1024]{1,0:T(8,128)(2,1)S(1)} %convolution_convert_fusion, bf16[1024,3,512]{2,0,1:T(8,128)(2,1)S(1)} %copy-done.3), kind=kOutput, calls=%fused_computation.7 | convolution fusion | flops 536870912 | bytes 3145728 | tf_op jit(solution)/shard_map/dot_general | solution.py:297
  18.6 3.5 %fusion.8.key_ref = f32[1536,512]{1,0:T(8,128)} fusion(bf16[1536,1024]{1,0:T(8,128)(2,1)S(1)} %convolution_convert_fusion, bf16[1024,3,512]{2,0,1:T(8,128)(2,1)S(1)} %copy-done.3), kind=kOutput, calls=%fused_computation.10 | convolution fusion | flops 1610612736 | bytes 7340032 | tf_op jit(solution)/shard_map/dot_general | solution.py:298
  22.1 0.0 copy-done.1
  22.1 3.0 %convolution_convert_fusion.1.value_ref = bf16[1536,512]{1,0:T(8,128)(2,1)} fusion(bf16[1536,1024]{1,0:T(8,128)(2,1)S(1)} %convolution_convert_fusion, bf16[1024,3,512]{2,0,1:T(8,128)(2,1)S(1)} %copy-done.3), kind=kOutput, calls=%fused_computation.2 | convolution fusion | flops 1611399168 | bytes 5767168 | tf_op jit(solution)/shard_map/dot_general | solution.py:299
  25.1 23.8 %window_attend.1 = bf16[512,512]{1,0:T(8,128)(2,1)} custom-call(s32[8,2]{1,0:T(8,128)} %copy.178.shift_ref, f32[8]{0:T(128)} %scale_ref.1, s32[2]{0:T(128)} %pad_add_fusion.3.band_ref, f32[512,512]{1,0:T(8,128)} %fusion.5.query_ref, f32[1536,512]{1,0:T(8,128)} %fusion.8.key_ref, bf16[1536,512]{1,0:T(8,128)(2,1)} %convolution_convert_fusion.1.value_ref), custom_call_target="tpu_custom_call" | custom-call | tf_op jit(solution)/shard_map/window_attend/pallas_call | solution.py:107
  48.9 1.6 %convolution_bitcast_fusion.1 = f32[2,4,8,128]{3,2,1,0:T(8,128)S(1)} fusion(f32[512,16]{0,1:T(8,128)S(1)} %fusion.119, bf16[512,512]{1,0:T(8,128)(2,1)} %window_attend.1), kind=kOutput, calls=%fused_computation.6 | convolution fusion | flops 50331648 | bytes 589824 | tf_op jit(solution)/shard_map/mc,rm->cr/dot_general | solution.py:307
  50.5 1.9 %collective-permute-start.5 = (f32[16,2,128]{2,0,1:T(8,128)S(1)}, f32[16,2,128]{2,0,1:T(8,128)S(1)}, u32[]{:S(2)}, u32[]{:S(2)}) collective-permute-start(f32[16,2,128]{2,0,1:T(8,128)S(1)} %get-tuple-element.14), channel_id=1, source_target_pairs={{2,0},{3,1},{4,2},{5,3},{6,4},{7,5},{8,6},{9,7},{10,8},{11,9},{12,... | collective-permute-start | bytes 49160 | tf_op jit(solution)/shard_map/ppermute | solution.py:257
  52.4 2.8 %collective-permute-start.6 = (f32[16,2,128]{2,0,1:T(8,128)S(1)}, f32[16,2,128]{2,0,1:T(8,128)S(1)}, u32[]{:S(2)}, u32[]{:S(2)}) collective-permute-start(f32[16,2,128]{2,0,1:T(8,128)S(1)} %get-tuple-element.14), channel_id=1, source_target_pairs={{2,1},{3,0},{4,3},{5,2},{6,5},{7,4},{8,7},{9,6},{10,9},{11,8},{12,... | collective-permute-start | bytes 49160 | tf_op jit(solution)/shard_map/ppermute | solution.py:257
  55.2 0.4 collective-permute-start.4
  55.6 4.8 %collective-permute-start.2 = (f32[16,2,128]{2,0,1:T(8,128)S(1)}, f32[16,2,128]{2,0,1:T(8,128)S(1)}, u32[]{:S(2)}, u32[]{:S(2)}) collective-permute-start(f32[16,2,128]{2,0,1:T(8,128)S(1)} %get-tuple-element.13), channel_id=1, source_target_pairs={{0,2},{1,3},{2,4},{3,5},{4,6},{5,7},{6,8},{7,9},{8,10},{9,11},{10,... | collective-permute-start | bytes 49160 | tf_op jit(solution)/shard_map/ppermute | solution.py:257
  60.5 3.2 %collective-permute-start.3 = (f32[16,2,128]{2,0,1:T(8,128)S(1)}, f32[16,2,128]{2,0,1:T(8,128)S(1)}, u32[]{:S(2)}, u32[]{:S(2)}) collective-permute-start(f32[16,2,128]{2,0,1:T(8,128)S(1)} %get-tuple-element.13), channel_id=1, source_target_pairs={{0,3},{1,2},{2,5},{3,4},{4,7},{5,6},{6,9},{7,8},{8,11},{9,10},{10,... | collective-permute-start | bytes 49160 | tf_op jit(solution)/shard_map/ppermute | solution.py:257
  63.7 0.0 copy-done.2
  63.7 2.2 %fusion.2 = f32[2,8,8,128]{3,2,1,0:T(8,128)S(1)} fusion(bf16[1024,16]{0,1:T(8,128)(2,1)S(1)} %copy-done.2, bf16[1536,1024]{1,0:T(8,128)(2,1)} %copy-done.1), kind=kOutput, calls=%fused_computation.5 | convolution fusion | flops 33554432 | bytes 2195456 | tf_op jit(solution)/shard_map/dc,rd->cr/dot_general | solution.py:315
  65.9 0.0 collective-permute-done.5
  65.9 0.0 collective-permute-done.6
  65.9 0.0 collective-permute-done.2
  65.9 0.0 collective-permute-done.3
  66.0 0.0 collective-permute-done.4
  66.0 0.1 fusion.107
  66.1 0.2 copy.184
  66.3 0.0 copy-done.4
  66.3 1.6 %fusion.118 = f32[1,6,66,512]{3,0,2,1:T(1,128)S(1)} fusion(bf16[1,8,68,16]{3,0,2,1:T(2,128)(2,1)S(1)} %copy.184, bf16[3,3,16,512]{3,2,1,0:T(8,128)(2,1)S(1)} %copy-done.4), kind=kOutput, calls=%fused_computation.217 | convolution fusion | flops 58392576 | bytes 975872 | tf_op jit(solution)/shard_map/conv_general_dilated | solution.py:190
  67.9 0.3 fusion.28
  68.2 0.9 pad_bitcast_fusion.field_ref
  69.1 0.1 pad_slice_fusion
  69.2 0.8 pad_maximum_fusion.2.turned_ref
  70.0 10.1 %grow.3 = bf16[2,5,2,80,512]{4,3,2,1,0:T(8,128)(2,1)} custom-call(s32[2]{0:T(128)} %pad_add_fusion.2.base_ref, bf16[1,6,80,512]{3,2,1,0:T(8,128)(2,1)} %pad_bitcast_fusion.field_ref, bf16[6,80,512]{2,1,0:T(8,128)(2,1)} %pad_maximum_fusion.2.turned_ref, bf16[3,3,512,512]{3,2,1,0:T(8,128)(2,1)} %weight_ref.3), custom_call_target="tpu_custom_call" | custom-call | tf_op jit(solution)/shard_map/grow/pallas_call | solution.py:177
  80.2 1.2 slice.367
  81.4 0.2 slice.368
  81.6 1.0 pad_maximum_fusion.turned_ref
  82.6 12.3 %grow.4 = bf16[4,9,2,80,256]{4,3,2,1,0:T(8,128)(2,1)} custom-call(s32[2]{0:T(128)} %pad_add_fusion.1.base_ref, bf16[2,10,80,512]{3,2,1,0:T(8,128)(2,1)} %bitcast.518, bf16[10,80,512]{2,1,0:T(8,128)(2,1)} %pad_maximum_fusion.turned_ref, bf16[3,3,512,256]{3,2,1,0:T(8,128)(2,1)} %weight_ref.4), custom_call_target="tpu_custom_call" | custom-call | tf_op jit(solution)/shard_map/grow/pallas_call | solution.py:177
  94.8 1.2 slice.370
  96.0 0.3 slice.371
  96.3 1.0 pad_maximum_fusion.1.turned_ref
  97.3 13.1 %grow.5 = bf16[8,17,2,80,128]{4,3,2,1,0:T(8,128)(2,1)} custom-call(s32[2]{0:T(128)} %pad_add_fusion.base_ref, bf16[4,18,80,256]{3,2,1,0:T(8,128)(2,1)} %bitcast.517, bf16[18,80,256]{2,1,0:T(8,128)(2,1)} %pad_maximum_fusion.1.turned_ref, bf16[3,3,256,128]{3,2,1,0:T(8,128)(2,1)} %weight_ref.5), custom_call_target="tpu_custom_call" | custom-call | tf_op jit(solution)/shard_map/grow/pallas_call | solution.py:177
  110.4 7.8 %convolution_bitcast_fusion = f32[36,21760]{1,0:T(8,128)} fusion(bf16[21760,128]{1,0:T(8,128)(2,1)} %bitcast.516, bf16[36,128]{1,0:T(8,128)(2,1)S(1)} %reshape.103), kind=kOutput, calls=%fused_computation | convolution fusion | flops 200540160 | bytes 8713216 | tf_op jit(solution)/shard_map/dot_general | solution.py:213
  118.2 6.8 %reshape.104 = f32[3,3,4,8,34,80]{5,4,3,2,1,0:T(8,128)} reshape(f32[36,21760]{1,0:T(8,128)} %convolution_bitcast_fusion) | data formatting | bytes 6266880 | tf_op jit(solution)/shard_map/reshape | solution.py:218
  125.1 1.5 %fusion.78 = (f32[4,32,64]{2,1,0:T(8,128)S(1)}, f32[4,32,64]{2,1,0:T(8,128)S(1)}) fusion(f32[3,3,4,8,34,80]{5,4,3,2,1,0:T(8,128)} %reshape.104), kind=kLoop, calls=%fused_computation.135 | loop fusion | flops 131072 | bytes 655360 | tf_op jit(solution)/shard_map/add | solution.py:225
  126.6 1.5 %fusion.51 = (f32[4,32,64]{2,1,0:T(8,128)S(1)}, f32[4,32,64]{2,1,0:T(8,128)S(1)}) fusion(f32[3,3,4,8,34,80]{5,4,3,2,1,0:T(8,128)} %reshape.104), kind=kLoop, calls=%fused_computation.81 | loop fusion | flops 131072 | bytes 655360 | tf_op jit(solution)/shard_map/add | solution.py:225
  128.1 1.5 %fusion.60 = (f32[4,32,64]{2,1,0:T(8,128)S(1)}, f32[4,32,64]{2,1,0:T(8,128)S(1)}) fusion(f32[3,3,4,8,34,80]{5,4,3,2,1,0:T(8,128)} %reshape.104), kind=kLoop, calls=%fused_computation.99 | loop fusion | flops 131072 | bytes 655360 | tf_op jit(solution)/shard_map/add | solution.py:225
  129.6 1.6 %fusion.33 = (f32[4,32,64]{2,1,0:T(8,128)S(1)}, f32[4,32,64]{2,1,0:T(8,128)S(1)}) fusion(f32[3,3,4,8,34,80]{5,4,3,2,1,0:T(8,128)} %reshape.104), kind=kLoop, calls=%fused_computation.45 | loop fusion | flops 131072 | bytes 655360 | tf_op jit(solution)/shard_map/add | solution.py:225
  131.2 0.2 concatenate.34
  131.4 1.5 %fusion.15 = f32[4,32,512]{2,1,0:T(8,128)} fusion(f32[4,32,512]{2,1,0:T(8,128)S(1)} %concatenate.34, s32[512]{0:T(512)S(1)} %get-tuple-element.15, s32[512]{0:T(512)S(1)} %get-tuple-element.18, s32[512]{0:T(512)S(1)} %get-tuple-element.16, s32[512]{0:T(512)S(1)} %get-tuple-element.17, pred[512]{0:T(512)(128)(4,1)S(1)} %get-tuple-element.19, ...), kind=kOutput, calls=%fused_computation.18 | convolution fusion | flops 403963904 | bytes 533504 | tf_op jit(solution)/shard_map/vrs,st->vrt/dot_general | solution.py:231
  (21 shorter events, 0.2 us)
Async XLA Ops:
  0.0 10.0 %copy-start = (bf16[512,1024]{1,0:T(8,128)(2,1)S(1)}, bf16[512,1024]{1,0:T(8,128)(2,1)}, u32[]{:S(2)}) copy-start(bf16[512,1024]{1,0:T(8,128)(2,1)} %param.21) | copy-start | bytes 3145732
  1.5 13.0 %collective-permute-start.1 = (bf16[17,4,128]{2,0,1:T(8,128)(2,1)S(1)}, bf16[17,4,128]{2,0,1:T(8,128)(2,1)S(1)}, u32[]{:S(2)}, u32[]{:S(2)}) collective-permute-start(bf16[17,4,128]{2,0,1:T(8,128)(2,1)S(1)} %constant_dynamic-update-slice_fusion), channel_id=1, source_target_pairs={{2,0},{4,2},{6,4},{8,6},{10,8},{12,10},{14,12},{16,14},{18,16},{20... | collective-permute-start | bytes 52232 | tf_op jit(solution)/shard_map/ppermute | solution.py:28
  4.1 10.4 %collective-permute-start = (bf16[17,4,128]{2,0,1:T(8,128)(2,1)S(1)}, bf16[17,4,128]{2,0,1:T(8,128)(2,1)S(1)}, u32[]{:S(2)}, u32[]{:S(2)}) collective-permute-start(bf16[17,4,128]{2,0,1:T(8,128)(2,1)S(1)} %constant_dynamic-update-slice_fusion), channel_id=1, source_target_pairs={{0,2},{2,4},{4,6},{6,8},{8,10},{10,12},{12,14},{14,16},{16,18},{18... | collective-permute-start | bytes 52232 | tf_op jit(solution)/shard_map/ppermute | solution.py:27
  14.5 2.1 %copy-start.3 = (bf16[1024,3,512]{2,0,1:T(8,128)(2,1)S(1)}, bf16[1024,3,512]{2,0,1:T(8,128)(2,1)}, u32[]{:S(2)}) copy-start(bf16[1024,3,512]{2,0,1:T(8,128)(2,1)} %param.20) | copy-start | bytes 9437188
  16.6 5.5 %copy-start.1 = (bf16[1536,1024]{1,0:T(8,128)(2,1)}, bf16[1536,1024]{1,0:T(8,128)(2,1)S(1)}, u32[]{:S(2)}) copy-start(bf16[1536,1024]{1,0:T(8,128)(2,1)S(1)} %convolution_convert_fusion) | copy-start | bytes 9437188
  25.1 38.6 %copy-start.2 = (bf16[1024,16]{0,1:T(8,128)(2,1)S(1)}, bf16[1024,16]{0,1:T(8,128)(2,1)}, u32[]{:S(2)}) copy-start(bf16[1024,16]{0,1:T(8,128)(2,1)} %param.22) | copy-start | bytes 98308
  48.9 17.4 %copy-start.4 = (bf16[3,3,16,512]{3,2,1,0:T(8,128)(2,1)S(1)}, bf16[3,3,16,512]{3,2,1,0:T(8,128)(2,1)}, u32[]{:S(2)}) copy-start(bf16[3,3,16,512]{3,2,1,0:T(8,128)(2,1)} %param.23) | copy-start | bytes 442372
  50.5 15.4 %collective-permute-start.5 = (f32[16,2,128]{2,0,1:T(8,128)S(1)}, f32[16,2,128]{2,0,1:T(8,128)S(1)}, u32[]{:S(2)}, u32[]{:S(2)}) collective-permute-start(f32[16,2,128]{2,0,1:T(8,128)S(1)} %get-tuple-element.14), channel_id=1, source_target_pairs={{2,0},{3,1},{4,2},{5,3},{6,4},{7,5},{8,6},{9,7},{10,8},{11,9},{12,... | collective-permute-start | bytes 49160 | tf_op jit(solution)/shard_map/ppermute | solution.py:257
  52.4 13.5 %collective-permute-start.6 = (f32[16,2,128]{2,0,1:T(8,128)S(1)}, f32[16,2,128]{2,0,1:T(8,128)S(1)}, u32[]{:S(2)}, u32[]{:S(2)}) collective-permute-start(f32[16,2,128]{2,0,1:T(8,128)S(1)} %get-tuple-element.14), channel_id=1, source_target_pairs={{2,1},{3,0},{4,3},{5,2},{6,5},{7,4},{8,7},{9,6},{10,9},{11,8},{12,... | collective-permute-start | bytes 49160 | tf_op jit(solution)/shard_map/ppermute | solution.py:257
  55.2 10.8 %collective-permute-start.4 = (f32[16,4,128]{2,0,1:T(8,128)S(1)}, f32[16,4,128]{2,0,1:T(8,128)S(1)}, u32[]{:S(2)}, u32[]{:S(2)}) collective-permute-start(f32[16,4,128]{2,0,1:T(8,128)S(1)} %bitcast.526), channel_id=1, source_target_pairs={{0,1},{1,0},{2,3},{3,2},{4,5},{5,4},{6,7},{7,6},{8,9},{9,8},{10,11... | collective-permute-start | bytes 98312 | tf_op jit(solution)/shard_map/ppermute | solution.py:257
  55.6 10.3 %collective-permute-start.2 = (f32[16,2,128]{2,0,1:T(8,128)S(1)}, f32[16,2,128]{2,0,1:T(8,128)S(1)}, u32[]{:S(2)}, u32[]{:S(2)}) collective-permute-start(f32[16,2,128]{2,0,1:T(8,128)S(1)} %get-tuple-element.13), channel_id=1, source_target_pairs={{0,2},{1,3},{2,4},{3,5},{4,6},{5,7},{6,8},{7,9},{8,10},{9,11},{10,... | collective-permute-start | bytes 49160 | tf_op jit(solution)/shard_map/ppermute | solution.py:257
  60.5 5.5 %collective-permute-start.3 = (f32[16,2,128]{2,0,1:T(8,128)S(1)}, f32[16,2,128]{2,0,1:T(8,128)S(1)}, u32[]{:S(2)}, u32[]{:S(2)}) collective-permute-start(f32[16,2,128]{2,0,1:T(8,128)S(1)} %get-tuple-element.13), channel_id=1, source_target_pairs={{0,3},{1,2},{2,5},{3,4},{4,7},{5,6},{6,9},{7,8},{8,11},{9,10},{10,... | collective-permute-start | bytes 49160 | tf_op jit(solution)/shard_map/ppermute | solution.py:257

commit v3 on v2

--- a/solution.py
+++ b/solution.py
@@ -125,7 +125,7 @@
     )(shifts, scales, band, query, key, value)
 
 
-def grow_kernel(phases, row_total, col_total, base_ref, field_ref, turned_ref, weight_ref, out_ref, taps):
+def grow_kernel(phases, row_total, col_total, base_ref, field_ref, weight_ref, out_ref, taps):
     odd = pl.program_id(0)
     depth, width = weight_ref.shape[2], weight_ref.shape[3]
     rows, stride = out_ref.shape[1], out_ref.shape[3]
@@ -154,9 +154,14 @@
     row_in = (row_index >= 0) & (row_index < row_total)
     for p in range(phases):
         def near(a):
-            here = field_ref[p, a : a + rows]
-            after = field_ref[p + 1, a : a + rows] if p < phases - 1 else turned_ref[a : a + rows]
-            return [piece.reshape(rows * stride, depth) for piece in (here, after)]
+            here = field_ref[p, a : a + rows].reshape(rows * stride, depth)
+            if p < phases - 1:
+                after = field_ref[p + 1, a : a + rows].reshape(rows * stride, depth)
+            else:
+                after = field_ref[0, a : a + rows].reshape(rows * stride, depth)
+                after = pltpu.roll(after.astype(jnp.float32), rows * stride - 1, 0)
+                after = after.astype(jnp.bfloat16)
+            return [here, after]
 
         lhs = jnp.concatenate(near(0) + near(1), axis=1)
         total = jnp.dot(lhs, taps[...], preferred_element_type=jnp.float32)
@@ -172,17 +177,16 @@
 def grow(field_in, weight, base, row_total, col_total):
     phases, rows, stride, depth = field_in.shape
     width = weight.shape[3]
-    turned = jnp.roll(field_in[0], -1, axis=1)
     whole = pl.BlockSpec(memory_space=pltpu.VMEM)
     out = pl.pallas_call(
         functools.partial(grow_kernel, phases, row_total, col_total),
         out_shape=jax.ShapeDtypeStruct((2 * phases, rows - 1, 2, stride, width), jnp.bfloat16),
         grid=(2,),
-        in_specs=[pl.BlockSpec(memory_space=pltpu.SMEM), whole, whole, whole],
+        in_specs=[pl.BlockSpec(memory_space=pltpu.SMEM), whole, whole],
         out_specs=pl.BlockSpec((2 * phases, rows - 1, 1, stride, width), lambda i: (0, 0, i, 0, 0)),
         scratch_shapes=[pltpu.VMEM((4 * depth, 2 * width), jnp.bfloat16)],
         name="grow",
-    )(base, field_in, turned, weight)
+    )(base, field_in, weight)
     return out.reshape(2 * phases, 2 * (rows - 1), stride, width)
 
 
@@ -210,12 +214,8 @@
     out_vars = weight.shape[3]
     steps = cols // phases
     taps = jnp.transpose(weight, (0, 1, 3, 2)).reshape(9 * out_vars, depth)
-    parts = lax.dot_general(
-        taps,
-        field_in.reshape(phases * rows_in * stride, depth),
-        (((1,), (1,)), ((), ())),
-        preferred_element_type=jnp.float32,
-    ).reshape(3, 3, out_vars, phases, rows_in, stride)
+    parts = jnp.einsum("kd,prsd->kprs", taps, field_in, preferred_element_type=jnp.float32)
+    parts = parts.reshape(3, 3, out_vars, phases, rows_in, stride)
     strips = []
     for q in range(phases):
         strip = jnp.zeros((out_vars, rows, steps), jnp.float32)
@@ -234,30 +234,13 @@
 
 
 def noise_everywhere(part):
-    wide = lax.axis_size("wide")
     narrow = lax.axis_size("narrow")
-    rows = part.shape[1]
-    pieces = {
-        1: lax.slice_in_dim(part, rows - HALO, rows, axis=1),
-        0: part,
-        -1: lax.slice_in_dim(part, 0, HALO, axis=1),
-    }
-    sums = {}
-    for move in (0, 1, -1):
-        total = part if move == 0 else None
-        for turn in range(narrow):
-            if move == 0 and turn == 0:
-                continue
-            pairs = [
-                (w * narrow + n, (w + move) * narrow + (n + turn) % narrow)
-                for w in range(wide)
-                for n in range(narrow)
-                if 0 <= w + move < wide
-            ]
-            arrived = lax.ppermute(pieces[move], ("wide", "narrow"), pairs)
-            total = arrived if total is None else total + arrived
-        sums[move] = total
-    return jnp.concatenate([sums[1], sums[0], sums[-1]], axis=1)
+    total = part
+    for turn in range(1, narrow):
+        total = total + lax.ppermute(
+            part, "narrow", [(n, (n + turn) % narrow) for n in range(narrow)]
+        )
+    return neighbour_rows(total, HALO, 1)
 
 
 def shards(

time: 134 us -> 118 us (0.88)
  other arithmetic: 12.6 us -> 3.9 us
  starting transfers between devices: 19.6 us -> 14.7 us
  local copies, waits for them, and re-layouts: 14.8 us -> 11.6 us
  waiting for transfers between devices: 0.03 us -> 2.55 us
    ppermute x5 -> x1, starting transfers between devices: 13.1 us -> 1.28 us  [noise_everywhere(): lax.ppermute(part, 'narrow', [(n, (n + turn) % narrow) for n in range(nar...]
    reshape x1 -> x0, local copies, waits for them, and re-layouts: 6.83 us -> none  [conv_final(): parts = lax.dot_general(taps, field_in.reshape(phases * rows_in * stride,...]
    add x4, other arithmetic: 6.14 us -> 0.41 us  [conv_final(): strip = strip + parts[a, b, :, p, a:a + rows, skip:skip + steps]]
    ppermute x1 -> x2, starting transfers between devices: 3.88 us -> 9.39 us  [neighbour_rows(): above = lax.ppermute(tail, 'wide', [(i, i + 1) for i in range(count - 1)])]
    concatenate x3 -> x0, other arithmetic: 2.83 us -> none  [grow(): turned = jnp.roll(field_in[0], -1, axis=1)]
    slice x9 -> x5, local copies, waits for them, and re-layouts: 3.01 us -> 5.73 us  [the longest x4 5.72 us: conv_final(): strip = strip + parts[a, b, :, p, a:a + rows, skip:skip + steps]]
    dot_general x0 -> x1, local copies, waits for them, and re-layouts: none -> 1.62 us  [conv_final(): jnp.einsum('kd,prsd->kprs', taps, field_in, preferred_element_type=jnp.fl...]
    ppermute x1 -> x2, waiting for transfers between devices: 0.01 us -> 1.6 us  [neighbour_rows(): below = lax.ppermute(head, 'wide', [(i + 1, i) for i in range(count - 1)])]
  transfers between devices with their start and end apart: 7 -> 5, of which waited for: 0 -> 2; matrix products, arithmetic and copies ran while one was open for 7% -> 7% of each run, Pallas kernels for 0% -> 0%
where the time goes in v3:
time: 118 us; the launch traced here: 117 us
  Pallas kernels  58.9 us (50%)
  matrix products  25.2 us (21%)
  starting transfers between devices  14.7 us (12%)
  local copies, waits for them, and re-layouts  11.6 us (10%)
  other arithmetic  3.9 us (3%)
  waiting for transfers between devices  2.55 us (2%)
    pallas_call x3, Pallas kernels, grow(): pl.pallas_call(functools.partial(grow_kernel, phases, row_total, col_tota...  35.1 us
    pallas_call x1, Pallas kernels, window_attend(): pl.pallas_call(functools.partial(attend_kernel, row_count, col_count, hea...  23.8 us
    ppermute x2, starting transfers between devices, neighbour_rows(): above = lax.ppermute(tail, 'wide', [(i, i + 1) for i in range(count - 1)])  9.39 us
    dot_general x1, matrix products, conv_final(): jnp.einsum('kd,prsd->kprs', taps, field_in, preferred_element_type=jnp.fl...  7.03 us
    slice x4, local copies, waits for them, and re-layouts, conv_final(): strip = strip + parts[a, b, :, p, a:a + rows, skip:skip + steps]  5.72 us
    ppermute x2, starting transfers between devices, neighbour_rows(): below = lax.ppermute(head, 'wide', [(i + 1, i) for i in range(count - 1)])  4.02 us
    dot_general x1, matrix products, shards(): jnp.dot(embedded, qkv_weight[:, 1], preferred_element_type=jnp.float32)  3.48 us
    dot_general x1, matrix products, shards(): jnp.dot(embedded, qkv_weight[:, 2], preferred_element_type=jnp.float32)  2.98 us
  transfers between devices with their start and end apart: 5, of which 2 were waited for; matrix products, arithmetic and copies ran while one was open for 7% of the time, Pallas kernels for 0%

profile of v3, /device:TPU:21, one launch (start us, length us, event | category | flops | bytes accessed | tf_op | source)
XLA Modules:
  0.0 117.1 jit_solution(9246729550793744483)
XLA Ops:
  0.0 0.0 copy-start
  0.0 0.8 copy_dynamic-update-slice_fusion
  0.8 0.7 convert_bitcast_fusion
  1.5 3.7 %collective-permute-start = (bf16[17,4,128]{2,0,1:T(8,128)(2,1)S(1)}, bf16[17,4,128]{2,0,1:T(8,128)(2,1)S(1)}, u32[]{:S(2)}, u32[]{:S(2)}) collective-permute-start(bf16[17,4,128]{2,0,1:T(8,128)(2,1)S(1)} %constant_dynamic-update-slice_fusion), channel_id=1, source_target_pairs={{0,2},{2,4},{4,6},{6,8},{8,10},{10,12},{12,14},{14,16},{16,18},{18... | collective-permute-start | bytes 52232 | tf_op jit(solution)/shard_map/ppermute | solution.py:27
  5.2 1.9 %collective-permute-start.1 = (bf16[17,4,128]{2,0,1:T(8,128)(2,1)S(1)}, bf16[17,4,128]{2,0,1:T(8,128)(2,1)S(1)}, u32[]{:S(2)}, u32[]{:S(2)}) collective-permute-start(bf16[17,4,128]{2,0,1:T(8,128)(2,1)S(1)} %constant_dynamic-update-slice_fusion), channel_id=1, source_target_pairs={{2,0},{4,2},{6,4},{8,6},{10,8},{12,10},{14,12},{16,14},{18,16},{20... | collective-permute-start | bytes 52232 | tf_op jit(solution)/shard_map/ppermute | solution.py:28
  7.2 0.6 pad_add_fusion.3.band_ref
  7.9 0.0 copy-done
  7.9 1.1 fusion.52
  9.0 0.1 broadcast_and_fusion
  9.1 0.6 pad_add_fusion.2.base_ref
  9.7 0.6 pad_add_fusion.1.base_ref
  10.3 0.7 broadcast_in_dim.28
  11.0 1.3 %copy.175.shift_ref = s32[8,2]{1,0:T(8,128)} copy(s32[8,2]{0,1:T(2,128)} %param.16) | data formatting | bytes 128 | tf_op args[2]
  12.3 0.0 copy-start.4
  12.3 0.0 collective-permute-done
  12.3 0.0 collective-permute-done.1
  12.4 1.9 %convolution_convert_fusion = bf16[1536,1024]{1,0:T(8,128)(2,1)S(1)} fusion(bf16[17,1536]{1,0:T(8,128)(2,1)S(1)} %bitcast.181, bf16[1,1024]{1,0:T(2,128)(2,1)S(1)} %broadcast_in_dim.28, bf16[16,1024]{1,0:T(8,128)(2,1)} %param.18), kind=kOutput, calls=%fused_computation | convolution fusion | flops 55119872 | bytes 3232768 | tf_op jit(solution)/shard_map/cm,cd->md/dot_general | solution.py:273
  14.3 0.0 copy-done.4
  14.3 0.0 copy-start.1
  14.4 3.5 %fusion.8.key_ref = f32[1536,512]{1,0:T(8,128)} fusion(bf16[1536,1024]{1,0:T(8,128)(2,1)S(1)} %convolution_convert_fusion, bf16[1024,3,512]{2,0,1:T(8,128)(2,1)S(1)} %copy-done.4), kind=kOutput, calls=%fused_computation.10 | convolution fusion | flops 1610612736 | bytes 7340032 | tf_op jit(solution)/shard_map/dot_general | solution.py:281
  17.8 3.0 %convolution_convert_fusion.1.value_ref = bf16[1536,512]{1,0:T(8,128)(2,1)} fusion(bf16[1536,1024]{1,0:T(8,128)(2,1)S(1)} %convolution_convert_fusion, bf16[1024,3,512]{2,0,1:T(8,128)(2,1)S(1)} %copy-done.4), kind=kOutput, calls=%fused_computation.1 | convolution fusion | flops 1611399168 | bytes 5767168 | tf_op jit(solution)/shard_map/dot_general | solution.py:282
  20.8 0.0 copy-done.1
  20.8 1.8 %fusion.5.query_ref = f32[512,512]{1,0:T(8,128)} fusion(bf16[1536,1024]{1,0:T(8,128)(2,1)S(1)} %convolution_convert_fusion, bf16[1024,3,512]{2,0,1:T(8,128)(2,1)S(1)} %copy-done.4), kind=kOutput, calls=%fused_computation.7 | convolution fusion | flops 536870912 | bytes 3145728 | tf_op jit(solution)/shard_map/dot_general | solution.py:280
  22.6 0.0 copy-start.3
  22.6 0.0 copy-start.2
  22.6 23.8 %window_attend.1 = bf16[512,512]{1,0:T(8,128)(2,1)} custom-call(s32[8,2]{1,0:T(8,128)} %copy.175.shift_ref, f32[8]{0:T(128)} %scale_ref.1, s32[2]{0:T(128)} %pad_add_fusion.3.band_ref, f32[512,512]{1,0:T(8,128)} %fusion.5.query_ref, f32[1536,512]{1,0:T(8,128)} %fusion.8.key_ref, bf16[1536,512]{1,0:T(8,128)(2,1)} %convolution_convert_fusion.1.value_ref), custom_call_target="tpu_custom_call" | custom-call | tf_op jit(solution)/shard_map/window_attend/pallas_call | solution.py:107
  46.4 0.0 copy-start.5
  46.4 1.6 %convolution_bitcast_fusion.1 = f32[2,4,8,128]{3,2,1,0:T(8,128)S(1)} fusion(f32[512,16]{0,1:T(8,128)S(1)} %fusion.52, bf16[512,512]{1,0:T(8,128)(2,1)} %window_attend.1), kind=kOutput, calls=%fused_computation.6 | convolution fusion | flops 50331648 | bytes 589824 | tf_op jit(solution)/shard_map/mc,rm->cr/dot_general | solution.py:290
  48.0 1.3 %collective-permute-start.2 = (f32[16,4,128]{2,0,1:T(8,128)S(1)}, f32[16,4,128]{2,0,1:T(8,128)S(1)}, u32[]{:S(2)}, u32[]{:S(2)}) collective-permute-start(f32[16,4,128]{2,0,1:T(8,128)S(1)} %bitcast.254), channel_id=1, source_target_pairs={{0,1},{1,0},{2,3},{3,2},{4,5},{5,4},{6,7},{7,6},{8,9},{9,8},{10,11... | collective-permute-start | bytes 98312 | tf_op jit(solution)/shard_map/ppermute | solution.py:240
  49.2 0.6 pad_add_fusion.base_ref
  49.8 0.0 copy-done.3
  49.8 0.9 collective-permute-done.2
  50.8 5.7 %collective-permute-start.3 = (f32[16,2,128]{2,0,1:T(8,128)S(1)}, f32[16,2,128]{2,0,1:T(8,128)S(1)}, u32[]{:S(2)}, u32[]{:S(2)}) collective-permute-start(f32[16,2,128]{2,0,1:T(8,128)S(1)} %get-tuple-element.77), channel_id=1, source_target_pairs={{0,2},{2,4},{4,6},{6,8},{8,10},{10,12},{12,14},{14,16},{16,18},{18... | collective-permute-start | bytes 49160 | tf_op jit(solution)/shard_map/ppermute | solution.py:27
  56.5 2.1 %collective-permute-start.4 = (f32[16,2,128]{2,0,1:T(8,128)S(1)}, f32[16,2,128]{2,0,1:T(8,128)S(1)}, u32[]{:S(2)}, u32[]{:S(2)}) collective-permute-start(f32[16,2,128]{2,0,1:T(8,128)S(1)} %get-tuple-element.78), channel_id=1, source_target_pairs={{2,0},{4,2},{6,4},{8,6},{10,8},{12,10},{14,12},{16,14},{18,16},{20... | collective-permute-start | bytes 49160 | tf_op jit(solution)/shard_map/ppermute | solution.py:28
  58.6 0.0 copy-done.2
  58.6 2.2 %fusion.2 = f32[2,8,8,128]{3,2,1,0:T(8,128)S(1)} fusion(bf16[1024,16]{0,1:T(8,128)(2,1)S(1)} %copy-done.2, bf16[1536,1024]{1,0:T(8,128)(2,1)} %copy-done.1), kind=kOutput, calls=%fused_computation.5 | convolution fusion | flops 33554432 | bytes 2195456 | tf_op jit(solution)/shard_map/dc,rd->cr/dot_general | solution.py:298
  60.9 0.0 collective-permute-done.3
  60.9 1.6 %collective-permute-done.4 = f32[16,2,128]{2,0,1:T(8,128)S(1)} collective-permute-done((f32[16,2,128]{2,0,1:T(8,128)S(1)}, f32[16,2,128]{2,0,1:T(8,128)S(1)}, u32[]{:S(2)}, u32[]{:S(2)}) %collective-permute-start.4) | collective-permute-done | bytes 16416 | tf_op jit(solution)/shard_map/ppermute | solution.py:28
  62.5 0.1 fusion.35
  62.6 0.2 copy.179
  62.8 0.0 copy-done.5
  62.8 1.6 %fusion.51 = f32[1,6,66,512]{3,0,2,1:T(1,128)S(1)} fusion(bf16[1,8,68,16]{3,0,2,1:T(2,128)(2,1)S(1)} %copy.179, bf16[3,3,16,512]{3,2,1,0:T(8,128)(2,1)S(1)} %copy-done.5), kind=kOutput, calls=%fused_computation.82 | convolution fusion | flops 58392576 | bytes 975872 | tf_op jit(solution)/shard_map/conv_general_dilated | solution.py:194
  64.4 0.3 fusion.28
  64.6 0.8 pad_bitcast_fusion.field_ref
  65.5 10.0 %grow.3 = bf16[2,5,2,80,512]{4,3,2,1,0:T(8,128)(2,1)} custom-call(s32[2]{0:T(128)} %pad_add_fusion.2.base_ref, bf16[1,6,80,512]{3,2,1,0:T(8,128)(2,1)} %pad_bitcast_fusion.field_ref, bf16[3,3,512,512]{3,2,1,0:T(8,128)(2,1)} %weight_ref.3), custom_call_target="tpu_custom_call" | custom-call | tf_op jit(solution)/shard_map/grow/pallas_call | solution.py:181
  75.5 12.0 %grow.4 = bf16[4,9,2,80,256]{4,3,2,1,0:T(8,128)(2,1)} custom-call(s32[2]{0:T(128)} %pad_add_fusion.1.base_ref, bf16[2,10,80,512]{3,2,1,0:T(8,128)(2,1)} %bitcast.179, bf16[3,3,512,256]{3,2,1,0:T(8,128)(2,1)} %weight_ref.4), custom_call_target="tpu_custom_call" | custom-call | tf_op jit(solution)/shard_map/grow/pallas_call | solution.py:181
  87.5 13.1 %grow.5 = bf16[8,17,2,80,128]{4,3,2,1,0:T(8,128)(2,1)} custom-call(s32[2]{0:T(128)} %pad_add_fusion.base_ref, bf16[4,18,80,256]{3,2,1,0:T(8,128)(2,1)} %bitcast.178, bf16[3,3,256,128]{3,2,1,0:T(8,128)(2,1)} %weight_ref.5), custom_call_target="tpu_custom_call" | custom-call | tf_op jit(solution)/shard_map/grow/pallas_call | solution.py:181
  100.6 7.0 %convolution_bitcast_fusion = f32[36,8,34,80]{3,0,2,1:T(8,128)S(1)} fusion(bf16[8,34,80,128]{3,2,1,0:T(8,128)(2,1)} %bitcast.173, bf16[36,128,1,1]{1,0,2,3:T(8,128)(2,1)S(1)} %reshape.137), kind=kOutput, calls=%fused_computation.2 | convolution fusion | flops 200540160 | bytes 8713216 | tf_op jit(solution)/shard_map/kd,prsd->kprs/dot_general | solution.py:217
  107.6 1.6 %copy.180 = f32[36,8,34,80]{3,1,2,0:T(8,128)S(1)} copy(f32[36,8,34,80]{3,0,2,1:T(8,128)S(1)} %convolution_bitcast_fusion) | data formatting | bytes 6266880 | tf_op jit(solution)/shard_map/kd,prsd->kprs/dot_general | solution.py:217
  109.3 1.9 %fusion.46 = (f32[1,1,4,1,32,64]{5,3,4,2,1,0:T(1,128)S(1)}, f32[1,1,4,1,32,64]{5,3,4,2,1,0:T(1,128)S(1)}, f32[1,1,4,1,32,64]{5,3,4,2,1,0:T(1,128)S(1)}, f32[1,1,...) fusion(f32[3,3,4,8,34,80]{5,3,4,2,1,0:T(8,128)S(1)} %bitcast.174), kind=kLoop, calls=%fused_computation.77 | loop fusion | bytes 1245184 | tf_op jit(solution)/shard_map/slice | solution.py:225
  111.2 1.5 %fusion.47 = (f32[1,1,4,1,32,64]{5,3,4,2,1,0:T(1,128)S(1)}, f32[1,1,4,1,32,64]{5,3,4,2,1,0:T(1,128)S(1)}, f32[1,1,4,1,32,64]{5,3,4,2,1,0:T(1,128)S(1)}, f32[1,1,...) fusion(f32[3,3,4,8,34,80]{5,3,4,2,1,0:T(8,128)S(1)} %bitcast.175), kind=kLoop, calls=%fused_computation.78 | loop fusion | bytes 1245184 | tf_op jit(solution)/shard_map/slice | solution.py:225
  112.6 1.4 %fusion.48 = (f32[1,1,4,1,32,64]{5,3,4,2,1,0:T(1,128)S(1)}, f32[1,1,4,1,32,64]{5,3,4,2,1,0:T(1,128)S(1)}, f32[1,1,4,1,32,64]{5,3,4,2,1,0:T(1,128)S(1)}, f32[1,1,...) fusion(f32[3,3,4,8,34,80]{5,3,4,2,1,0:T(8,128)S(1)} %bitcast.176), kind=kLoop, calls=%fused_computation.79 | loop fusion | bytes 1245184 | tf_op jit(solution)/shard_map/slice | solution.py:225
  114.1 0.9 fusion.49
  115.0 0.1 add_bitcast_fusion
  115.1 0.1 add_bitcast_fusion.2
  115.2 0.1 add_bitcast_fusion.4
  115.3 0.1 add_bitcast_fusion.6
  115.4 0.2 concatenate.19
  115.6 1.5 %fusion.15 = f32[4,32,512]{2,1,0:T(8,128)} fusion(f32[4,32,512]{2,1,0:T(8,128)S(1)} %concatenate.19, s32[512]{0:T(512)S(1)} %get-tuple-element.87, s32[512]{0:T(512)S(1)} %get-tuple-element.90, s32[512]{0:T(512)S(1)} %get-tuple-element.88, s32[512]{0:T(512)S(1)} %get-tuple-element.89, pred[512]{0:T(512)(128)(4,1)S(1)} %get-tuple-element.91, ...), kind=kOutput, calls=%fused_computation.18 | convolution fusion | flops 403963904 | bytes 533504 | tf_op jit(solution)/shard_map/vrs,st->vrt/dot_general | solution.py:231
  (15 shorter events, 0.2 us)
Async XLA Ops:
  0.0 7.9 %copy-start = (bf16[512,1024]{1,0:T(8,128)(2,1)S(1)}, bf16[512,1024]{1,0:T(8,128)(2,1)}, u32[]{:S(2)}) copy-start(bf16[512,1024]{1,0:T(8,128)(2,1)} %param.21) | copy-start | bytes 3145732
  1.5 10.8 %collective-permute-start = (bf16[17,4,128]{2,0,1:T(8,128)(2,1)S(1)}, bf16[17,4,128]{2,0,1:T(8,128)(2,1)S(1)}, u32[]{:S(2)}, u32[]{:S(2)}) collective-permute-start(bf16[17,4,128]{2,0,1:T(8,128)(2,1)S(1)} %constant_dynamic-update-slice_fusion), channel_id=1, source_target_pairs={{0,2},{2,4},{4,6},{6,8},{8,10},{10,12},{12,14},{14,16},{16,18},{18... | collective-permute-start | bytes 52232 | tf_op jit(solution)/shard_map/ppermute | solution.py:27
  5.2 7.1 %collective-permute-start.1 = (bf16[17,4,128]{2,0,1:T(8,128)(2,1)S(1)}, bf16[17,4,128]{2,0,1:T(8,128)(2,1)S(1)}, u32[]{:S(2)}, u32[]{:S(2)}) collective-permute-start(bf16[17,4,128]{2,0,1:T(8,128)(2,1)S(1)} %constant_dynamic-update-slice_fusion), channel_id=1, source_target_pairs={{2,0},{4,2},{6,4},{8,6},{10,8},{12,10},{14,12},{16,14},{18,16},{20... | collective-permute-start | bytes 52232 | tf_op jit(solution)/shard_map/ppermute | solution.py:28
  12.3 2.0 %copy-start.4 = (bf16[1024,3,512]{2,0,1:T(8,128)(2,1)S(1)}, bf16[1024,3,512]{2,0,1:T(8,128)(2,1)}, u32[]{:S(2)}) copy-start(bf16[1024,3,512]{2,0,1:T(8,128)(2,1)} %param.20) | copy-start | bytes 9437188
  14.3 6.5 %copy-start.1 = (bf16[1536,1024]{1,0:T(8,128)(2,1)}, bf16[1536,1024]{1,0:T(8,128)(2,1)S(1)}, u32[]{:S(2)}) copy-start(bf16[1536,1024]{1,0:T(8,128)(2,1)S(1)} %convolution_convert_fusion) | copy-start | bytes 9437188
  22.6 27.3 %copy-start.3 = (bf16[3,3,128,4]{2,3,1,0:T(4,128)(2,1)S(1)}, bf16[3,3,128,4]{2,3,1,0:T(4,128)(2,1)}, u32[]{:S(2)}) copy-start(bf16[3,3,128,4]{2,3,1,0:T(4,128)(2,1)} %param.27) | copy-start | bytes 27652
  22.6 36.1 %copy-start.2 = (bf16[1024,16]{0,1:T(8,128)(2,1)S(1)}, bf16[1024,16]{0,1:T(8,128)(2,1)}, u32[]{:S(2)}) copy-start(bf16[1024,16]{0,1:T(8,128)(2,1)} %param.22) | copy-start | bytes 98308
  46.4 16.4 %copy-start.5 = (bf16[3,3,16,512]{3,2,1,0:T(8,128)(2,1)S(1)}, bf16[3,3,16,512]{3,2,1,0:T(8,128)(2,1)}, u32[]{:S(2)}) copy-start(bf16[3,3,16,512]{3,2,1,0:T(8,128)(2,1)} %param.23) | copy-start | bytes 442372
  48.0 2.8 %collective-permute-start.2 = (f32[16,4,128]{2,0,1:T(8,128)S(1)}, f32[16,4,128]{2,0,1:T(8,128)S(1)}, u32[]{:S(2)}, u32[]{:S(2)}) collective-permute-start(f32[16,4,128]{2,0,1:T(8,128)S(1)} %bitcast.254), channel_id=1, source_target_pairs={{0,1},{1,0},{2,3},{3,2},{4,5},{5,4},{6,7},{7,6},{8,9},{9,8},{10,11... | collective-permute-start | bytes 98312 | tf_op jit(solution)/shard_map/ppermute | solution.py:240
  50.8 10.1 %collective-permute-start.3 = (f32[16,2,128]{2,0,1:T(8,128)S(1)}, f32[16,2,128]{2,0,1:T(8,128)S(1)}, u32[]{:S(2)}, u32[]{:S(2)}) collective-permute-start(f32[16,2,128]{2,0,1:T(8,128)S(1)} %get-tuple-element.77), channel_id=1, source_target_pairs={{0,2},{2,4},{4,6},{6,8},{8,10},{10,12},{12,14},{14,16},{16,18},{18... | collective-permute-start | bytes 49160 | tf_op jit(solution)/shard_map/ppermute | solution.py:27
  56.5 6.0 %collective-permute-start.4 = (f32[16,2,128]{2,0,1:T(8,128)S(1)}, f32[16,2,128]{2,0,1:T(8,128)S(1)}, u32[]{:S(2)}, u32[]{:S(2)}) collective-permute-start(f32[16,2,128]{2,0,1:T(8,128)S(1)} %get-tuple-element.78), channel_id=1, source_target_pairs={{2,0},{4,2},{6,4},{8,6},{10,8},{12,10},{14,12},{16,14},{18,16},{20... | collective-permute-start | bytes 49160 | tf_op jit(solution)/shard_map/ppermute | solution.py:28
